TPU v7x, 32 devices: a whole 2x2x4 slice. The times are simulated.
32 devices in a mesh: tm: 8 (over z, x), user: 4 (over y, core).
Axes of the slice: x: 2, y: 2, z: 4, core: 2. Of those that a mesh axis runs over, the one named last changes fastest.
Arguments:
- user_factor: bfloat16 [8192, 128], P('user'), may hold values from -2.390625 to 2.390625
- user_tangent: bfloat16 [8192, 128], P('user'), may hold values from -2.390625 to 2.390625
- item_factor: bfloat16 [512, 128], P('tm'), may hold values from -2.390625 to 2.390625
- item_tangent: bfloat16 [512, 128], P('tm'), may hold values from -2.390625 to 2.390625
- time_factor: bfloat16 [128, 128], P('tm'), may hold values from -2.390625 to 2.390625
- time_tangent: bfloat16 [128, 128], P('tm'), may hold values from -2.390625 to 2.390625
- send_list: int32 [8, 4, 4, 4], P('tm', 'user'), may hold values from 0 to 15
- tile_slot: int32 [8, 4, 16], P('tm', 'user'), may hold values from 0 to 15, as said below
- tile_item: int32 [8, 4, 16], P('tm', 'user'), may hold values from 0 to 1
- tile_count: int32 [8, 4], P('tm', 'user'), may hold values from 8 to 16, as said below
Outputs:
- user_hvp: float32 [8192, 128], P('user')
- item_hvp: float32 [512, 128], P('tm')
- time_hvp: float32 [128, 128], P('tm')
Inputs may be any that keep to these rules, and one draw needn't show every extreme that they name: `tile_slot`: for each (a, j) the first min(16, 16) entries are distinct. `tile_count`: some pair (a, j) has exactly 16 tiles in every draw.
All inputs are finite; a program needn't handle non-finite values.
Results may differ from a plain program's by a relative error of at most 0.0013.
Values may be sent and summed in bfloat16 or wider, within the bound.
No kernel may reach another device: no remote copies, remote signals or barrier semaphores. Data moves between devices by JAX's collectives and lax.ppermute only.
A program may use at most 64 MiB of HBM per device.

v0:
```python
import jax
import jax.numpy as jnp
from jax import lax
from jax.sharding import PartitionSpec as P

R = 128
UB = 128
IT = 256
NT_CAP = 16


OBS_WEIGHT = 0.03125
LAMBDA_USER = 0.5
LAMBDA_ITEM = 0.5
LAMBDA_TIME = 1.0


def with_halo(cells, sides, width):
    for axis, dim in sides:
        count = lax.axis_size(axis)
        ends = count - 1
        head = lax.slice_in_dim(cells, 0, width, axis=dim)
        tail = lax.slice_in_dim(cells, cells.shape[dim] - width, cells.shape[dim], axis=dim)
        cells = jnp.concatenate(
            [
                lax.ppermute(tail, axis, [(i, (i + 1) % count) for i in range(ends)]),
                cells,
                lax.ppermute(head, axis, [((i + 1) % count, i) for i in range(ends)]),
            ],
            axis=dim,
        )
    return cells


def tile_terms(user_block, user_delta, item_block, item_delta, time_rows, time_delta):
    factor_u = user_block.astype(jnp.float32)
    delta_u = user_delta.astype(jnp.float32)
    scaled = (factor_u[None] * time_rows[:, None, :]).astype(jnp.bfloat16)
    mixed = (
        delta_u[None] * time_rows[:, None, :] + factor_u[None] * time_delta[:, None, :]
    ).astype(jnp.bfloat16)
    left_side = jnp.concatenate([mixed, scaled], axis=-1)
    right_side = jnp.concatenate([item_block, item_delta], axis=-1)
    change = jnp.einsum(
        "tuk,ik->tui", left_side, right_side, preferred_element_type=jnp.float32
    ).astype(jnp.bfloat16)
    projected = jnp.einsum("tui,ir->tur", change, item_block, preferred_element_type=jnp.float32)
    user_term = jnp.sum(projected * time_rows[:, None, :], axis=0)
    time_term = jnp.sum(projected * factor_u[None], axis=1)
    item_term = jnp.einsum("tui,tur->ir", change, scaled, preferred_element_type=jnp.float32)
    return (user_term, item_term, time_term)


def add_tile(
    number,
    carry,
    weight,
    slot_blocks,
    slot_deltas,
    all_items,
    all_deltas,
    time_rows,
    time_delta,
    slots,
    item_ids,
):
    slot_acc, item_acc, time_acc = carry
    where = slots[number]
    which = item_ids[number] * IT
    user_block = lax.dynamic_index_in_dim(slot_blocks, where, 0, keepdims=False)
    user_delta = lax.dynamic_index_in_dim(slot_deltas, where, 0, keepdims=False)
    item_block = lax.dynamic_slice_in_dim(all_items, which, IT, 0)
    item_delta = lax.dynamic_slice_in_dim(all_deltas, which, IT, 0)
    user_term, item_term, time_term = tile_terms(
        user_block, user_delta, item_block, item_delta, time_rows, time_delta
    )
    slot_acc = slot_acc.at[where].add(weight * user_term)
    current = lax.dynamic_slice_in_dim(item_acc, which, IT, 0)
    item_acc = lax.dynamic_update_slice_in_dim(item_acc, current + weight * item_term, which, 0)
    time_acc = time_acc + weight * time_term
    return (slot_acc, item_acc, time_acc)


def body(
    user_factor,
    user_tangent,
    item_factor,
    item_tangent,
    time_factor,
    time_tangent,
    send_list,
    tile_slot,
    tile_item,
    tile_count,
):
    all_items, all_deltas = (
        lax.all_gather(item_factor, "tm", axis=0, tiled=True),
        lax.all_gather(item_tangent, "tm", axis=0, tiled=True),
    )
    block_rows = user_factor.shape[0] // UB
    peers = lax.axis_size("user")
    home_blocks = user_factor.reshape(block_rows, UB, R)
    home_deltas = user_tangent.reshape(block_rows, UB, R)
    chosen = send_list[0, 0]
    got_blocks, got_deltas = (
        lax.all_to_all(home_blocks[chosen], "user", split_axis=0, concat_axis=0, tiled=True),
        lax.all_to_all(home_deltas[chosen], "user", split_axis=0, concat_axis=0, tiled=True),
    )
    slot_blocks = got_blocks.reshape(-1, UB, R)
    slot_deltas = got_deltas.reshape(-1, UB, R)
    time_rows = time_factor.astype(jnp.float32)
    time_delta = time_tangent.astype(jnp.float32)
    slots = tile_slot[0, 0]
    item_ids = tile_item[0, 0]
    count = tile_count[0, 0]
    start = (
        jnp.zeros(slot_blocks.shape, jnp.float32),
        jnp.zeros(all_items.shape, jnp.float32),
        jnp.zeros(time_rows.shape, jnp.float32),
    )

    def padded_tile(number, carry):
        weight = OBS_WEIGHT * (number < count).astype(jnp.float32)
        return add_tile(
            number,
            carry,
            weight,
            slot_blocks,
            slot_deltas,
            all_items,
            all_deltas,
            time_rows,
            time_delta,
            slots,
            item_ids,
        )

    slot_acc, item_acc, time_acc = lax.fori_loop(0, NT_CAP, padded_tile, start)
    returned = lax.all_to_all(
        slot_acc.reshape(peers, -1, UB, R), "user", split_axis=0, concat_axis=0, tiled=True
    )
    flat_ids = send_list[0, 0].reshape(-1)
    table = (jnp.arange(block_rows, dtype=jnp.int32)[:, None] == flat_ids[None, :]).astype(
        jnp.float32
    )
    home_grads = jnp.dot(
        table,
        returned.reshape(flat_ids.shape[0], -1),
        precision=lax.Precision.HIGHEST,
        preferred_element_type=jnp.float32,
    ).reshape(-1, R)
    user_hvp = lax.psum(home_grads, "tm") + LAMBDA_USER * user_tangent.astype(jnp.float32)
    piece = lax.psum_scatter(item_acc, "tm", scatter_dimension=0, tiled=True)
    piece, time_acc = lax.psum((piece, time_acc), "user")
    item_hvp = piece + LAMBDA_ITEM * item_tangent.astype(jnp.float32)
    steps_here = time_tangent.shape[0]
    extended = with_halo(time_tangent, (("tm", 0),), 2).astype(jnp.float32)
    second = extended[:-2] - 2.0 * extended[1:-1] + extended[2:]
    position = lax.axis_index("tm") * steps_here - 1 + jnp.arange(steps_here + 2, dtype=jnp.int32)
    total_steps = steps_here * lax.axis_size("tm")
    interior = (position >= 1) & (position <= total_steps - 2)
    second = jnp.where(interior[:, None], second, 0.0)
    penalty = second[:-2] - 2.0 * second[1:-1] + second[2:]
    time_hvp = time_acc + LAMBDA_TIME * penalty
    return (user_hvp, item_hvp, time_hvp)


def solution(mesh):
    return jax.shard_map(
        body,
        mesh=mesh,
        in_specs=(
            P("user", None),
            P("user", None),
            P("tm", None),
            P("tm", None),
            P("tm", None),
            P("tm", None),
            P("tm", "user", None, None),
            P("tm", "user", None),
            P("tm", "user", None),
            P("tm", "user"),
        ),
        out_specs=(P("user", None), P("tm", None), P("tm", None)),
        check_vma=False,
    )
```

profile of v0, /device:TPU:1, one launch (start us, length us, event | category | flops | bytes accessed | tf_op | source)
XLA Modules:
  0.0 425.8 jit_solution(17418752064839015805)
XLA Ops:
  8.0 2.4 gather_fusion
  10.5 4.3 %all-to-all-start = ((bf16[4,4,128,128]{3,2,1,0:T(8,128)(2,1)}), bf16[4,4,128,128]{3,2,1,0:T(8,128)(2,1)S(1)}, u32[]{:S(2)}, u32[]{:S(2)}) async-start(bf16[4,4,128,128]{3,2,1,0:T(8,128)(2,1)} %bitcast.4), calls=%async_computation | async-start | bytes 1048576 | tf_op jit(solution)/shard_map/all_to_all | solution.py:107
  14.8 1.4 gather_fusion.1
  16.2 6.3 %all-to-all-done = bf16[4,4,128,128]{3,2,1,0:T(8,128)(2,1)S(1)} async-done(((bf16[4,4,128,128]{3,2,1,0:T(8,128)(2,1)}), bf16[4,4,128,128]{3,2,1,0:T(8,128)(2,1)S(1)}, u32[]{:S(2)}, u32[]{:S(2)}) %all-to-all-start) | async-done | bytes 524320 | tf_op jit(solution)/shard_map/all_to_all | solution.py:107
  22.4 4.6 %all-to-all-start.1 = ((bf16[4,4,128,128]{3,2,1,0:T(8,128)(2,1)}), bf16[4,4,128,128]{3,2,1,0:T(8,128)(2,1)S(1)}, u32[]{:S(2)}, u32[]{:S(2)}) async-start(bf16[4,4,128,128]{3,2,1,0:T(8,128)(2,1)} %bitcast.7), calls=%async_computation.1 | async-start | bytes 1048576 | tf_op jit(solution)/shard_map/all_to_all | solution.py:106
  27.1 25.2 %all_gather.6 = bf16[512,128]{1,0:T(8,128)(2,1)S(1)} all-gather(bf16[64,128]{1,0:T(8,128)(2,1)S(1)} %copy-done.5), channel_id=1, replica_groups=mesh['tm'=8,'user'=4] {'tm'}, dimensions={0}, use_global_device_ids=true | all-gather | bytes 147456 | tf_op jit(solution)/shard_map/all_gather | solution.py:97
  52.2 24.8 %all_gather.7 = bf16[512,128]{1,0:T(8,128)(2,1)S(1)} all-gather(bf16[64,128]{1,0:T(8,128)(2,1)S(1)} %copy-done.3), channel_id=1, replica_groups=mesh['tm'=8,'user'=4] {'tm'}, dimensions={0}, use_global_device_ids=true | all-gather | bytes 147456 | tf_op jit(solution)/shard_map/all_gather | solution.py:98
  78.2 173.7 %while.19 = (s32[]{:T(128)}, f32[16,128,128]{2,1,0:T(8,128)}, f32[512,128]{1,0:T(8,128)S(1)}, f32[16,128]{1,0:T(8,128)S(1)}, s32[16]{0:T(128)S(1)}, /*index=5*/s...) while((s32[]{:T(128)}, f32[16,128,128]{2,1,0:T(8,128)}, ...), condition=%wide.region_4.5_spmd.clone, body=%wide.region_0.4_spmd.clone.sunk | while | flops 543035392 | bytes 10945942 | solution.py:138
  85.2 2.1 fusion.31
  87.3 1.7 fusion.32
  96.0 2.1 fusion.31
  98.2 1.7 fusion.32
  106.9 2.1 fusion.31
  109.0 1.7 fusion.32
  117.8 2.1 fusion.31
  119.9 1.7 fusion.32
  128.6 2.1 fusion.31
  130.7 1.7 fusion.32
  139.5 2.1 fusion.31
  141.6 1.7 fusion.32
  150.3 2.1 fusion.31
  152.4 1.7 fusion.32
  161.2 2.1 fusion.31
  163.3 1.7 fusion.32
  172.0 2.1 fusion.31
  174.1 1.7 fusion.32
  182.9 2.1 fusion.31
  185.0 1.7 fusion.32
  193.7 2.1 fusion.31
  195.8 1.7 fusion.32
  204.6 2.1 fusion.31
  206.7 1.7 fusion.32
  215.4 2.1 fusion.31
  217.6 1.7 fusion.32
  226.3 2.1 fusion.31
  228.4 1.7 fusion.32
  237.2 2.1 fusion.31
  239.3 1.7 fusion.32
  248.0 2.1 fusion.31
  250.1 1.7 fusion.32
  252.6 15.7 %all-to-all-start.2 = ((f32[4,4,128,128]{3,2,1,0:T(8,128)}), f32[4,4,128,128]{3,2,1,0:T(8,128)S(1)}, u32[]{:S(2)}, u32[]{:S(2)}) async-start(f32[4,4,128,128]{3,2,1,0:T(8,128)} %bitcast.10), calls=%async_computation.2 | async-start | bytes 2097152 | tf_op jit(solution)/shard_map/all_to_all | solution.py:139
  269.1 12.6 %all-to-all-done.2 = f32[4,4,128,128]{3,2,1,0:T(8,128)S(1)} async-done(((f32[4,4,128,128]{3,2,1,0:T(8,128)}), f32[4,4,128,128]{3,2,1,0:T(8,128)S(1)}, u32[]{:S(2)}, u32[]{:S(2)}) %all-to-all-start.2) | async-done | bytes 1048608 | tf_op jit(solution)/shard_map/all_to_all | solution.py:139
  284.1 3.1 collective-permute-start
  288.5 3.4 collective-permute-done.1
  292.0 41.3 %reduce-scatter.2.cloned.1.call-done = f32[64,128]{1,0:T(8,128)} async-done(((f32[512,128]{1,0:T(8,128)}), f32[64,128]{1,0:T(8,128)}) %reduce-scatter.2.cloned.1.call-update) | async-done | bytes 32784 | tf_op jit(solution)/shard_map/reduce_scatter | solution.py:153
  333.3 13.6 %all-reduce = (f32[64,128]{1,0:T(8,128)S(1)}, f32[16,128]{1,0:T(8,128)S(1)}) all-reduce(f32[64,128]{1,0:T(8,128)} %reduce-scatter.2.cloned.1.call-done, f32[16,128]{1,0:T(8,128)S(1)} %get-tuple-element.243), channel_id=1, replica_groups=mesh['tm'=8,'user'=4] {'user'}, use_global_device_ids=true, to_apply=%region_7.8 | all-reduce | flops 10240 | bytes 81920 | tf_op jit(solution)/shard_map/psum | solution.py:154
  348.2 68.5 %all-reduce.3.cloned.1.call-done = f32[2048,128]{1,0:T(8,128)} async-done(((f32[2048,128]{1,0:T(8,128)}), f32[2048,128]{1,0:T(8,128)}) %all-reduce.3.cloned.1.call-update) | async-done | bytes 1048592 | tf_op jit(solution)/shard_map/psum | solution.py:152
  416.7 2.3 multiply_add_fusion
  (222 shorter events, 68.2 us)
Async XLA Ops:
  7.2 7.6 %copy-start = (bf16[2048,128]{1,0:T(8,128)(2,1)S(1)}, bf16[2048,128]{1,0:T(8,128)(2,1)}, u32[]{:S(2)}) copy-start(bf16[2048,128]{1,0:T(8,128)(2,1)} %param.14) | copy-start | bytes 1572868
  10.5 12.0 %all-to-all-start = ((bf16[4,4,128,128]{3,2,1,0:T(8,128)(2,1)}), bf16[4,4,128,128]{3,2,1,0:T(8,128)(2,1)S(1)}, u32[]{:S(2)}, u32[]{:S(2)}) async-start(bf16[4,4,128,128]{3,2,1,0:T(8,128)(2,1)} %bitcast.4), calls=%async_computation | async-start | bytes 1048576 | tf_op jit(solution)/shard_map/all_to_all | solution.py:107
  14.7 12.3 %copy-start.8 = (bf16[16,128]{1,0:T(8,128)(2,1)S(1)}, bf16[16,128]{1,0:T(8,128)(2,1)}, u32[]{:S(2)}) copy-start(bf16[16,128]{1,0:T(8,128)(2,1)} %param.18) | copy-start | bytes 12292
  14.7 12.3 %copy-start.4 = (bf16[16,128]{1,0:T(8,128)(2,1)S(1)}, bf16[16,128]{1,0:T(8,128)(2,1)}, u32[]{:S(2)}) copy-start(bf16[16,128]{1,0:T(8,128)(2,1)} %param.19) | copy-start | bytes 12292
  14.8 12.3 %copy-start.5 = (bf16[64,128]{1,0:T(8,128)(2,1)S(1)}, bf16[64,128]{1,0:T(8,128)(2,1)}, u32[]{:S(2)}) copy-start(bf16[64,128]{1,0:T(8,128)(2,1)} %param.16) | copy-start | bytes 49156
  14.8 37.5 %copy-start.3 = (bf16[64,128]{1,0:T(8,128)(2,1)S(1)}, bf16[64,128]{1,0:T(8,128)(2,1)}, u32[]{:S(2)}) copy-start(bf16[64,128]{1,0:T(8,128)(2,1)} %param.17) | copy-start | bytes 49156
  22.4 54.6 %all-to-all-start.1 = ((bf16[4,4,128,128]{3,2,1,0:T(8,128)(2,1)}), bf16[4,4,128,128]{3,2,1,0:T(8,128)(2,1)S(1)}, u32[]{:S(2)}, u32[]{:S(2)}) async-start(bf16[4,4,128,128]{3,2,1,0:T(8,128)(2,1)} %bitcast.7), calls=%async_computation.1 | async-start | bytes 1048576 | tf_op jit(solution)/shard_map/all_to_all | solution.py:106
  27.0 51.1 %copy-start.6 = (s32[3]{0:T(128)S(1)}, s32[3]{0:T(128)}, u32[]{:S(2)}) copy-start(s32[3]{0:T(128)} %constant.113.clone.2) | copy-start | bytes 40
  27.0 51.1 %copy-start.9 = (s32[1,1,16]{2,1,0:T(1,128)S(1)}, s32[1,1,16]{2,1,0:T(1,128)}, u32[]{:S(2)}) copy-start(s32[1,1,16]{2,1,0:T(1,128)} %param.21) | copy-start | bytes 196
  27.0 51.1 %copy-start.10 = (s32[1,1,16]{2,1,0:T(1,128)S(1)}, s32[1,1,16]{2,1,0:T(1,128)}, u32[]{:S(2)}) copy-start(s32[1,1,16]{2,1,0:T(1,128)} %param.22) | copy-start | bytes 196
  82.8 1.0 copy-start.11
  93.7 1.0 copy-start.11
  104.5 1.0 copy-start.11
  115.4 1.0 copy-start.11
  126.2 1.0 copy-start.11
  137.1 1.0 copy-start.11
  147.9 1.0 copy-start.11
  158.8 1.0 copy-start.11
  169.6 1.0 copy-start.11
  180.5 1.0 copy-start.11
  191.4 1.0 copy-start.11
  202.2 1.0 copy-start.11
  213.1 1.0 copy-start.11
  223.9 1.0 copy-start.11
  234.8 1.0 copy-start.11
  245.6 1.0 copy-start.11
  251.9 0.7 copy-start.2
  251.9 17.2 %copy-start.7 = (s32[1,1,4,4]{3,2,1,0:T(4,128)S(1)}, s32[1,1,4,4]{3,2,1,0:T(4,128)}, u32[]{:S(2)}) copy-start(s32[1,1,4,4]{3,2,1,0:T(4,128)} %param.20) | copy-start | bytes 196
  252.6 29.2 %all-to-all-start.2 = ((f32[4,4,128,128]{3,2,1,0:T(8,128)}), f32[4,4,128,128]{3,2,1,0:T(8,128)S(1)}, u32[]{:S(2)}, u32[]{:S(2)}) async-start(f32[4,4,128,128]{3,2,1,0:T(8,128)} %bitcast.10), calls=%async_computation.2 | async-start | bytes 2097152 | tf_op jit(solution)/shard_map/all_to_all | solution.py:139
  268.3 65.1 %reduce-scatter.2.cloned.1.call-start = ((), (), s32[]{:S(2)}) async-start(), calls=%async_computation.5 | async-start | bytes 294912 | tf_op jit(solution)/shard_map/reduce_scatter | solution.py:153
  269.0 147.7 %all-reduce.3.cloned.1.call-start = ((), (), s32[]{:S(2)}) async-start(), calls=%async_computation.4 | async-start | bytes 2097152 | tf_op jit(solution)/shard_map/psum | solution.py:152
  284.1 132.6 %copy-start.1 = (bf16[2048,128]{1,0:T(8,128)(2,1)S(1)}, bf16[2048,128]{1,0:T(8,128)(2,1)}, u32[]{:S(2)}) copy-start(bf16[2048,128]{1,0:T(8,128)(2,1)} %param.15) | copy-start | bytes 1572868
  284.1 4.4 %collective-permute-start = (bf16[2,128]{1,0:T(2,128)(2,1)S(1)}, bf16[2,128]{1,0:T(2,128)(2,1)S(1)}, u32[]{:S(2)}, u32[]{:S(2)}) collective-permute-start(bf16[2,128]{1,0:T(2,128)(2,1)S(1)} %get-tuple-element.322), channel_id=1, source_target_pairs={{0,4},{4,8},{8,12},{12,16},{16,20},{20,24},{24,28},{1,5},{5,9},{9,... | collective-permute-start | bytes 1544 | tf_op jit(solution)/shard_map/ppermute | solution.py:26
  287.2 4.7 %collective-permute-start.1 = (bf16[2,128]{1,0:T(2,128)(2,1)S(1)}, bf16[2,128]{1,0:T(2,128)(2,1)S(1)}, u32[]{:S(2)}, u32[]{:S(2)}) collective-permute-start(bf16[2,128]{1,0:T(2,128)(2,1)S(1)} %get-tuple-element.323), channel_id=1, source_target_pairs={{4,0},{8,4},{12,8},{16,12},{20,16},{24,20},{28,24},{5,1},{9,5},{13... | collective-permute-start | bytes 1544 | tf_op jit(solution)/shard_map/ppermute | solution.py:28
Sparse Core Ops, SparseCore 0:
  272.4 60.9 reduce-scatter.1
  337.4 79.1 all-reduce.2
where the time goes:
time: 429 us; the launch traced here: 426 us
  waiting for transfers between devices  133 us (31%)
  blocking collectives  63.6 us (15%)
  other arithmetic  55 us (13%)
  loops' own time  52.9 us (12%)
  matrix products  43.1 us (10%)
  local copies, waits for them, and re-layouts  35.3 us (8%)
  starting transfers between devices  28.9 us (7%)
  between operations  14.2 us (3%)
    psum x1, waiting for transfers between devices, body(): lax.psum(home_grads, 'tm') + LAMBDA_USER * user_tangent.astype(jnp.float32)  68.5 us
    another operation x1, loops' own time, body(): slot_acc, item_acc, time_acc = lax.fori_loop(0, NT_CAP, padded_tile, start)  52.9 us
    reduce_scatter x1, waiting for transfers between devices, body(): piece = lax.psum_scatter(item_acc, 'tm', scatter_dimension=0, tiled=True)  41.3 us
    scatter-add x16, other arithmetic, add_tile(): slot_acc = slot_acc.at[where].add(weight * user_term)  33.7 us
    dot_general x16, matrix products, tile_terms(): jnp.einsum('tui,tur->ir', change, scaled, preferred_element_type=jnp.floa...  27.3 us
    all_gather x1, blocking collectives, body(): lax.all_gather(item_factor, 'tm', axis=0, tiled=True)  25.2 us
    all_gather x1, blocking collectives, body(): lax.all_gather(item_tangent, 'tm', axis=0, tiled=True)  24.8 us
    all_to_all x1, starting transfers between devices, body(): lax.all_to_all(slot_acc.reshape(peers, -1, UB, R), 'user', split_axis=0,...  15.7 us
  transfers between devices with their start and end apart: 7, of which 5 were waited for; matrix products, arithmetic and copies ran while one was open for 1% of the time, Pallas kernels for 0%

commit v1 on v0

v1 whole, which is shorter than its diff:
```python
import functools

import jax
import jax.numpy as jnp
from jax import lax
from jax.experimental import pallas as pl
from jax.experimental.pallas import tpu as pltpu
from jax.sharding import PartitionSpec as P

R = 128
UB = 128
IT = 256
LANES = 128

OBS_WEIGHT = 0.03125
LAMBDA_USER = 0.5
LAMBDA_ITEM = 0.5
LAMBDA_TIME = 1.0

F32 = jnp.float32
BF16 = jnp.bfloat16
VM = pl.BlockSpec(memory_space=pltpu.VMEM)
SM = pl.BlockSpec(memory_space=pltpu.SMEM)


def iota(shape, dim):
    return lax.broadcasted_iota(jnp.int32, shape, dim)


def dot_tn(left, right):
    return lax.dot_general(left, right, (((0,), (0,)), ((), ())), preferred_element_type=F32)


def dot_nn(left, right):
    return lax.dot_general(left, right, (((1,), (0,)), ((), ())), preferred_element_type=F32)


def halves(values):
    high = values.astype(BF16)
    return high, (values - high.astype(F32)).astype(BF16)


def dot_split(left, right):
    both = dot_nn(left, jnp.concatenate(halves(right), axis=1))
    width = right.shape[1]
    return both[:, :width] + both[:, width:]


def pack_kernel(dims, v_ref, dv_ref, w_ref, dw_ref, send_ref, slot_ref, item_ref, count_ref, out_ref, time_ref):
    tm, peers, tiles, steps, rows = dims
    me = lax.axis_index("user")
    part = rows // peers
    start = pl.multiple_of(me * part, part)
    out_ref[0:part, :] = v_ref[pl.ds(start, part), :]
    out_ref[part : 2 * part, :] = dv_ref[pl.ds(start, part), :]
    time_ref[0:steps, :] = w_ref[...].astype(F32)
    time_ref[steps:, :] = dw_ref[...].astype(F32)
    piece = 2 * steps // peers
    time_rows = time_ref[pl.ds(pl.multiple_of(me * piece, piece), piece), :]
    slots = send_ref.shape[3]
    row, lane = iota((8, LANES), 0), iota((8, LANES), 1)
    wanted = row * slots + lane % slots
    table = jnp.full((8, LANES), -1, jnp.int32)
    count = count_ref[0, 0]
    for n in range(slot_ref.shape[2]):
        hit = (wanted == slot_ref[0, 0, n]) & (n < count)
        table = jnp.where(hit, item_ref[0, 0, n], table)
    entry = lane % (peers * slots)
    for j in range(peers):
        for s in range(slots):
            table = jnp.where((row == peers) & (entry == j * slots + s), send_ref[0, 0, j, s], table)
    out_ref[2 * part :, :] = jnp.concatenate([time_rows, table.astype(F32)], axis=0).astype(BF16)


def gram_kernel(u_ref, du_ref, out_ref):
    def one(g, carry):
        at = pl.ds(pl.multiple_of(g * UB, UB), UB)
        u = u_ref[at, :]
        out_ref[g] = dot_tn(jnp.concatenate([u, du_ref[at, :]], axis=1), u)
        return carry

    lax.fori_loop(0, out_ref.shape[0], one, 0)


def weighted(table, wt, ww):
    high, low = halves(wt * table)
    return dot_nn(jnp.concatenate([high, low], axis=1), ww)


def partial_kernel(dims, got_ref, gram_ref, v_ref, dv_ref, w_ref, dw_ref, out_ref, wt_ref, ww_ref, gh_ref, c_ref, own_ref):
    tm, peers, tiles, steps, rows = dims
    blocks = gram_ref.shape[0]
    part = rows // peers
    piece = 2 * steps // peers
    entries = LANES // steps
    chunks = tm // entries
    me_tm, me = lax.axis_index("tm"), lax.axis_index("user")
    lane, row8 = iota((8, LANES), 1), iota((8, LANES), 0)
    slots = steps // peers

    owner = iota((LANES, LANES), 0) // steps
    spread = (owner == iota((LANES, LANES), 1) // steps).astype(BF16)
    coeff_rows = me_tm * steps + iota((steps, LANES), 0)
    penalty = jnp.zeros((steps, R), F32)
    total_steps = tm * steps
    for chunk in range(chunks):
        base = chunk * entries
        pieces = []
        found_m = jnp.zeros((8, LANES), F32)
        found_g = jnp.zeros((8, LANES), F32)
        for a in range(entries):
            for j in range(peers):
                tile = got_ref[(base + a) * peers + j, 2 * part :, :].astype(F32)
                pieces.append(tile[:piece])
                mine = lane // steps == a
                hit = mine & (row8 == me) & (lane // slots % peers == j)
                found_m = found_m + jnp.where(hit, tile[piece:], 0.0)
                hit = mine & (row8 == peers) & (me == j)
                found_g = found_g + jnp.where(hit, tile[piece:], 0.0)
        half = peers // 2
        w = jnp.concatenate([pieces[a * peers + j] for a in range(entries) for j in range(half)], axis=0)
        dw = jnp.concatenate([pieces[a * peers + j] for a in range(entries) for j in range(half, peers)], axis=0)
        ww = w.astype(BF16)
        wt_ref[chunk] = jnp.concatenate([w, dw], axis=1).T
        ww_ref[chunk] = jnp.concatenate([ww, ww], axis=0)
        item = jnp.sum(found_m, axis=0, keepdims=True)
        block = jnp.sum(found_g, axis=0, keepdims=True)
        number = jnp.where(item < 0.0, -1.0, block * tiles + item).astype(jnp.int32)
        hot = (iota((blocks * tiles, LANES), 0) == number).astype(BF16)
        mine = (owner == me_tm - base).astype(BF16)
        counts = dot_nn(hot, jnp.concatenate([spread, mine], axis=1))
        c_ref[chunk] = counts[:, :LANES]
        own_ref[...] = counts[:, LANES:] + (own_ref[...] if chunk else 0.0)
        column = chunk * LANES + iota((steps, LANES), 1)
        coeff = jnp.zeros((steps, LANES), F32)
        for shift, scale in ((-1, 1.0), (0, -2.0), (1, 1.0)):
            centre = coeff_rows + shift
            inside = (centre >= 1) & (centre <= total_steps - 2)
            apart = column - centre
            value = jnp.where(apart == 0, -2.0, jnp.where(jnp.abs(apart) == 1, 1.0, 0.0))
            coeff = coeff + jnp.where(inside, scale * value, 0.0)
        penalty = penalty + dot_nn(coeff.astype(BF16), dw.astype(BF16))

    per_tile = IT // rows

    def item_grams(m, carry):
        def gathered(first):
            return jnp.concatenate(
                [got_ref[(m * per_tile + a) * peers + j, first : first + part, :] for a in range(per_tile) for j in range(peers)],
                axis=0,
            )

        v = gathered(0)
        gh_ref[m] = dot_tn(jnp.concatenate([v, gathered(part)], axis=1), v)
        return carry

    lax.fori_loop(0, tiles, item_grams, 0, unroll=tiles <= 2)

    def time_terms(m, carry):
        def add(g, total):
            return total + own_ref[pl.ds(g * tiles + m, 1), :] * gram_ref[g]

        total = lax.fori_loop(0, blocks, add, jnp.zeros((2 * R, R), F32), unroll=4)
        s, d = total[:R], total[R:]
        g_m, h_m = gh_ref[m, :R], gh_ref[m, R:]
        q, r = carry
        return q + d * g_m + s * h_m, r + s * g_m

    zero = jnp.zeros((R, R), F32)
    q, r = lax.fori_loop(0, tiles, time_terms, (zero, zero), unroll=tiles <= 2)
    left = jnp.concatenate([w_ref[...], dw_ref[...]], axis=1)
    time_rows = OBS_WEIGHT * dot_split(left, jnp.concatenate([q, r], axis=0))

    my_tile = me_tm * rows // IT

    def item_terms(g, carry):
        s, d = gram_ref[g, :R], gram_ref[g, R:]
        both = jnp.zeros((2 * R, R), F32)
        for chunk in range(chunks):
            both = both + weighted(c_ref[chunk, pl.ds(g * tiles + my_tile, 1), :], wt_ref[chunk], ww_ref[chunk])
        y, z = both[:R], both[R:]
        a, b = carry
        return a + d * y + s * z, b + s * y

    a, b = lax.fori_loop(0, blocks, item_terms, (zero, zero), unroll=2)
    left = jnp.concatenate([v_ref[...], dv_ref[...]], axis=1)
    item_rows = OBS_WEIGHT * dot_split(left, jnp.concatenate([a, b], axis=0))

    first = jnp.where(me == 0, 1.0, 0.0)
    out_ref[:rows, :] = item_rows + (first * LAMBDA_ITEM) * dv_ref[...].astype(F32)
    out_ref[rows:, :] = time_rows + (first * LAMBDA_TIME) * penalty


def user_kernel(dims, u_ref, du_ref, wt_ref, ww_ref, gh_ref, c_ref, out_ref):
    tm, peers, tiles, steps, rows = dims
    chunks = wt_ref.shape[0]

    def one(g, carry):
        def add(m, total):
            both = jnp.zeros((2 * R, R), F32)
            for chunk in range(chunks):
                both = both + weighted(c_ref[chunk, pl.ds(g * tiles + m, 1), :], wt_ref[chunk], ww_ref[chunk])
            y, z = both[:R], both[R:]
            g_m, h_m = gh_ref[m, :R], gh_ref[m, R:]
            return total[0] + g_m * y, total[1] + g_m * z + h_m * y

        zero = jnp.zeros((R, R), F32)
        k_delta, k_factor = lax.fori_loop(0, tiles, add, (zero, zero), unroll=tiles <= 2)
        at = pl.ds(pl.multiple_of(g * UB, UB), UB)
        du = du_ref[at, :]
        left = jnp.concatenate([du, u_ref[at, :]], axis=1)
        term = dot_split(left, jnp.concatenate([k_delta, k_factor], axis=0))
        out_ref[at, :] = OBS_WEIGHT * term + LAMBDA_USER * du.astype(F32)
        return carry

    lax.fori_loop(0, out_ref.shape[0] // UB, one, 0)


def shape(dims, dtype=F32):
    return jax.ShapeDtypeStruct(dims, dtype)


def body(user_factor, user_tangent, item_factor, item_tangent, time_factor, time_tangent, send_list, tile_slot, tile_item, tile_count):
    tm, peers = lax.axis_size("tm"), lax.axis_size("user")
    rows, steps = item_factor.shape[0], time_factor.shape[0]
    tiles = rows * tm // IT
    blocks = user_factor.shape[0] // UB
    dims = (tm, peers, tiles, steps, rows)
    chunks = tm * steps // LANES
    height = 2 * rows // peers + 2 * steps // peers + 8
    packed = pl.pallas_call(
        functools.partial(pack_kernel, dims),
        out_shape=shape((height, R), BF16),
        in_specs=[VM] * 4 + [SM] * 4,
        out_specs=VM,
        scratch_shapes=[pltpu.VMEM((2 * steps, R), F32)],
        name="pack",
    )(item_factor, item_tangent, time_factor, time_tangent, send_list, tile_slot, tile_item, tile_count)
    grams = pl.pallas_call(
        gram_kernel, out_shape=shape((blocks, 2 * R, R)), in_specs=[VM] * 2, out_specs=VM, name="grams"
    )(user_factor, user_tangent)
    got = lax.all_to_all(
        jnp.broadcast_to(packed[None], (tm * peers, height, R)), ("tm", "user"), split_axis=0, concat_axis=0, tiled=True
    )
    partial, wt, ww, gh, counts, _ = pl.pallas_call(
        functools.partial(partial_kernel, dims),
        out_shape=(
            shape((rows + steps, R)),
            shape((chunks, 2 * R, LANES)),
            shape((chunks, 2 * LANES, R), BF16),
            shape((tiles, 2 * R, R)),
            shape((chunks, blocks * tiles, LANES)),
            shape((blocks * tiles, LANES)),
        ),
        in_specs=[VM] * 6,
        out_specs=(VM,) * 6,
        name="partials",
    )(got, grams, item_factor, item_tangent, time_factor, time_tangent)
    step = 1
    while step < peers:
        partial = partial + lax.ppermute(partial, "user", [(i, i ^ step) for i in range(peers)])
        step *= 2
    user_hvp = pl.pallas_call(
        functools.partial(user_kernel, dims),
        out_shape=shape(user_factor.shape),
        in_specs=[VM] * 6,
        out_specs=VM,
        name="user_rows",
    )(user_factor, user_tangent, wt, ww, gh, counts)
    return (user_hvp, partial[:rows], partial[rows:])


def solution(mesh):
    return jax.shard_map(
        body,
        mesh=mesh,
        in_specs=(
            P("user", None),
            P("user", None),
            P("tm", None),
            P("tm", None),
            P("tm", None),
            P("tm", None),
            P("tm", "user", None, None),
            P("tm", "user", None),
            P("tm", "user", None),
            P("tm", "user"),
        ),
        out_specs=(P("user", None), P("tm", None), P("tm", None)),
        check_vma=False,
    )
```

time: 429 us -> 43.8 us (0.10)
  waiting for transfers between devices: 133 us -> 7.7 us
  blocking collectives: 63.6 us -> 0 us
  other arithmetic: 55 us -> 0.79 us
  loops' own time: 52.9 us -> 0 us
  matrix products: 43.1 us -> 0 us
  local copies, waits for them, and re-layouts: 35.3 us -> 3.47 us
  Pallas kernels: 0 us -> 20.9 us
  starting transfers between devices: 28.9 us -> 8.72 us
  between operations: 14.2 us -> 1.3 us
    psum x1 -> x0, waiting for transfers between devices: 68.5 us -> none  [body(): lax.psum(home_grads, 'tm') + LAMBDA_USER * user_tangent.astype(jnp.float32)]
    another operation x1 -> x0, loops' own time: 52.9 us -> none  [body(): slot_acc, item_acc, time_acc = lax.fori_loop(0, NT_CAP, padded_tile, start)]
    all_gather x2 -> x0, blocking collectives: 50 us -> none  [the longest x1 25.2 us: body(): lax.all_gather(item_factor, 'tm', axis=0, tiled=True)]
    dot_general x49 -> x0, matrix products: 43.1 us -> none  [the longest x16 27.3 us: tile_terms(): jnp.einsum('tui,tur->ir', change, scaled, preferred_element_type=jnp.floa...]
    reduce_scatter x1 -> x0, waiting for transfers between devices: 41.3 us -> none  [body(): piece = lax.psum_scatter(item_acc, 'tm', scatter_dimension=0, tiled=True)]
    scatter-add x16 -> x0, other arithmetic: 33.7 us -> none  [add_tile(): slot_acc = slot_acc.at[where].add(weight * user_term)]
    pallas_call x0 -> x4, Pallas kernels: none -> 20.9 us  [the longest x1 8.63 us: body(): pl.pallas_call(functools.partial(user_kernel, dims), out_shape=shape(user...]
    dynamic_slice x48 -> x0, local copies, waits for them, and re-layouts: 20 us -> none  [the longest x16 10.4 us: add_tile(): which = item_ids[number] * IT]
  transfers between devices with their start and end apart: 7 -> 3, of which waited for: 5 -> 2; matrix products, arithmetic and copies ran while one was open for 1% -> 0% of each run, Pallas kernels for 0% -> 33%
where the time goes in v1:
time: 43.8 us; the launch traced here: 42.9 us
  Pallas kernels  20.9 us (48%)
  starting transfers between devices  8.72 us (20%)
  waiting for transfers between devices  7.7 us (18%)
  local copies, waits for them, and re-layouts  3.47 us (8%)
  between operations  1.3 us (3%)
  other arithmetic  0.79 us (2%)
    pallas_call x1, Pallas kernels, body(): pl.pallas_call(functools.partial(user_kernel, dims), out_shape=shape(user...  8.63 us
    all_to_all x1, starting transfers between devices, body(): lax.all_to_all(jnp.broadcast_to(packed[None], (tm * peers, height, R)), (...  7.08 us
    all_to_all x1, waiting for transfers between devices, body(): lax.all_to_all(jnp.broadcast_to(packed[None], (tm * peers, height, R)), (...  6.62 us
    pallas_call x1, Pallas kernels, body(): pl.pallas_call(gram_kernel, out_shape=shape((blocks, 2 * R, R)), in_specs...  5.68 us
    pallas_call x1, Pallas kernels, body(): pl.pallas_call(functools.partial(partial_kernel, dims), out_shape=(shape(...  5.11 us
    ppermute x2, starting transfers between devices, body(): lax.ppermute(partial, 'user', [(i, i ^ step) for i in range(peers)])  1.64 us
    broadcast_in_dim x1, local copies, waits for them, and re-layouts, body(): jnp.broadcast_to(packed[None], (tm * peers, height, R))  1.5 us
    pallas_call x1, Pallas kernels, body(): pl.pallas_call(functools.partial(pack_kernel, dims), out_shape=shape((hei...  1.49 us
  transfers between devices with their start and end apart: 3, of which 2 were waited for; matrix products, arithmetic and copies ran while one was open for 0% of the time, Pallas kernels for 33%

profile of v1, /device:TPU:1, one launch (start us, length us, event | category | flops | bytes accessed | tf_op | source)
XLA Modules:
  0.0 42.9 jit_solution(8756616657133500721)
XLA Ops:
  1.3 1.5 %pack.1 = bf16[48,128]{1,0:T(8,128)(2,1)} custom-call(bf16[64,128]{1,0:T(8,128)(2,1)} %v_ref.3, bf16[64,128]{1,0:T(8,128)(2,1)} %dv_ref.3, bf16[16,128]{1,0:T(8,128)(2,1)} %w_ref.3, bf16[16,128]{1,0:T(8,128)(2,1)} %dw_ref.3, s32[1,1,4,4]{3,2,1,0:T(4,128)} %send_ref.1, s32[1,1,16]{2,1,0:T(1,128)} %slot_ref.1, s32[1,1,16]{2,1,0:T(1,128)} %item_ref.1, ...), custom_call_target="tpu_custom_call" | custom-call | tf_op jit(solution)/shard_map/pack/pallas_call | solution.py:231
  2.8 1.5 %broadcast_in_dim.2 = bf16[32,48,128]{2,1,0:T(8,128)(2,1)} broadcast(bf16[48,128]{1,0:T(8,128)(2,1)} %pack.1), dimensions={1,2} | broadcast | bytes 405504 | tf_op jit(solution)/shard_map/broadcast_in_dim | solution.py:243
  4.3 7.1 %all-to-all-start = ((bf16[32,48,128]{2,1,0:T(8,128)(2,1)}), bf16[32,48,128]{2,1,0:T(8,128)(2,1)S(1)}, u32[]{:S(2)}, u32[]{:S(2)}) async-start(bf16[32,48,128]{2,1,0:T(8,128)(2,1)} %broadcast_in_dim.2), calls=%async_computation | async-start | bytes 786432 | tf_op jit(solution)/shard_map/all_to_all | solution.py:242
  11.4 5.7 %grams.1.gram_ref = f32[16,256,128]{2,1,0:T(8,128)} custom-call(bf16[2048,128]{1,0:T(8,128)(2,1)} %u_ref.3, bf16[2048,128]{1,0:T(8,128)(2,1)} %du_ref.3), custom_call_target="tpu_custom_call" | custom-call | tf_op jit(solution)/shard_map/grams/pallas_call | solution.py:239
  17.0 6.6 %all-to-all-done.got_ref = bf16[32,48,128]{2,1,0:T(8,128)(2,1)S(1)} async-done(((bf16[32,48,128]{2,1,0:T(8,128)(2,1)}), bf16[32,48,128]{2,1,0:T(8,128)(2,1)S(1)}, u32[]{:S(2)}, u32[]{:S(2)}) %all-to-all-start) | async-done | bytes 393248 | tf_op jit(solution)/shard_map/all_to_all | solution.py:242
  23.7 0.0 copy-start
  23.7 0.7 %copy-done = bf16[32,48,128]{2,1,0:T(8,128)(2,1)} copy-done((bf16[32,48,128]{2,1,0:T(8,128)(2,1)}, bf16[32,48,128]{2,1,0:T(8,128)(2,1)S(1)}, u32[]{:S(2)}) %copy-start) | copy-done | bytes 393240
  24.4 5.1 %partials.1 = (f32[80,128]{1,0:T(8,128)}, f32[1,256,128]{2,1,0:T(8,128)}, bf16[1,256,128]{2,1,0:T(8,128)(2,1)}, f32[2,256,128]{2,1,0:T(8,128)}, f32[1,32,128]{2,1,0:T(8,128)}, /*index=5*/f32[32,128]{1,0:T(8,128)}) custom-call(bf16[32,48,128]{2,1,0:T(8,128)(2,1)} %copy-done, f32[16,256,128]{2,1,0:T(8,128)} %grams.1.gram_ref, bf16[64,128]{1,0:T(8,128)(2,1)} %v_ref.3, ...), custom_call_target="tpu_custom_call" | custom-call | tf_op jit(solution)/shard_map/partials/pallas_call | solution.py:245
  29.5 1.2 %collective-permute-start = (f32[80,128]{1,0:T(8,128)}, f32[80,128]{1,0:T(8,128)S(1)}, u32[]{:S(2)}, u32[]{:S(2)}) collective-permute-start(f32[80,128]{1,0:T(8,128)} %get-tuple-element.12), channel_id=1, source_target_pairs={{0,1},{1,0},{2,3},{3,2},{4,5},{5,4},{6,7},{7,6},{8,9},{9,8},{10,11... | collective-permute-start | bytes 122888 | tf_op jit(solution)/shard_map/ppermute | solution.py:261
  30.7 1.1 %collective-permute-done = f32[80,128]{1,0:T(8,128)S(1)} collective-permute-done((f32[80,128]{1,0:T(8,128)}, f32[80,128]{1,0:T(8,128)S(1)}, u32[]{:S(2)}, u32[]{:S(2)}) %collective-permute-start) | collective-permute-done | bytes 40992 | tf_op jit(solution)/shard_map/ppermute | solution.py:261
  31.8 0.8 %add.6 = f32[80,128]{1,0:T(8,128)S(1)} add(f32[80,128]{1,0:T(8,128)} %get-tuple-element.12, f32[80,128]{1,0:T(8,128)S(1)} %collective-permute-done) | non-fusion elementwise | flops 10240 | bytes 122880 | tf_op jit(solution)/shard_map/add | solution.py:261
  32.6 0.4 %collective-permute-start.1 = (f32[80,128]{1,0:T(8,128)S(1)}, f32[80,128]{1,0:T(8,128)S(1)}, u32[]{:S(2)}, u32[]{:S(2)}) collective-permute-start(f32[80,128]{1,0:T(8,128)S(1)} %add.6), channel_id=1, source_target_pairs={{0,2},{1,3},{2,0},{3,1},{4,6},{5,7},{6,4},{7,5},{8,10},{9,11},{10,... | collective-permute-start | bytes 122888 | tf_op jit(solution)/shard_map/ppermute | solution.py:261
  33.0 8.6 %user_rows.1 = f32[2048,128]{1,0:T(8,128)} custom-call(bf16[2048,128]{1,0:T(8,128)(2,1)} %u_ref.3, bf16[2048,128]{1,0:T(8,128)(2,1)} %du_ref.3, f32[1,256,128]{2,1,0:T(8,128)} %get-tuple-element.8.wt_ref, bf16[1,256,128]{2,1,0:T(8,128)(2,1)} %get-tuple-element.9.ww_ref, f32[2,256,128]{2,1,0:T(8,128)} %get-tuple-element.10.gh_ref, ...), custom_call_target="tpu_custom_call" | custom-call | tf_op jit(solution)/shard_map/user_rows/pallas_call | solution.py:263
  41.7 0.0 collective-permute-done.1
  41.7 0.6 %slice.9 = f32[16,128]{1,0:T(8,128)} slice(f32[80,128]{1,0:T(8,128)S(1)} %add.7), slice={[64:80], [0:128]} | slice | bytes 16384 | tf_op jit(solution)/shard_map/slice | solution.py:270
  42.3 0.6 %slice.8 = f32[64,128]{1,0:T(8,128)} slice(f32[80,128]{1,0:T(8,128)S(1)} %add.7), slice={[0:64], [0:128]} | slice | bytes 65536 | tf_op jit(solution)/shard_map/slice | solution.py:270
  (1 shorter events, 0.0 us)
Async XLA Ops:
  4.3 19.4 %all-to-all-start = ((bf16[32,48,128]{2,1,0:T(8,128)(2,1)}), bf16[32,48,128]{2,1,0:T(8,128)(2,1)S(1)}, u32[]{:S(2)}, u32[]{:S(2)}) async-start(bf16[32,48,128]{2,1,0:T(8,128)(2,1)} %broadcast_in_dim.2), calls=%async_computation | async-start | bytes 786432 | tf_op jit(solution)/shard_map/all_to_all | solution.py:242
  23.7 0.7 %copy-start = (bf16[32,48,128]{2,1,0:T(8,128)(2,1)}, bf16[32,48,128]{2,1,0:T(8,128)(2,1)S(1)}, u32[]{:S(2)}) copy-start(bf16[32,48,128]{2,1,0:T(8,128)(2,1)S(1)} %all-to-all-done.got_ref) | copy-start | bytes 1179652
  29.5 2.3 %collective-permute-start = (f32[80,128]{1,0:T(8,128)}, f32[80,128]{1,0:T(8,128)S(1)}, u32[]{:S(2)}, u32[]{:S(2)}) collective-permute-start(f32[80,128]{1,0:T(8,128)} %get-tuple-element.12), channel_id=1, source_target_pairs={{0,1},{1,0},{2,3},{3,2},{4,5},{5,4},{6,7},{7,6},{8,9},{9,8},{10,11... | collective-permute-start | bytes 122888 | tf_op jit(solution)/shard_map/ppermute | solution.py:261
  32.6 9.1 %collective-permute-start.1 = (f32[80,128]{1,0:T(8,128)S(1)}, f32[80,128]{1,0:T(8,128)S(1)}, u32[]{:S(2)}, u32[]{:S(2)}) collective-permute-start(f32[80,128]{1,0:T(8,128)S(1)} %add.6), channel_id=1, source_target_pairs={{0,2},{1,3},{2,0},{3,1},{4,6},{5,7},{6,4},{7,5},{8,10},{9,11},{10,... | collective-permute-start | bytes 122888 | tf_op jit(solution)/shard_map/ppermute | solution.py:261

commit v2 on v1

--- a/solution.py
+++ b/solution.py
@@ -51,8 +51,6 @@
     me = lax.axis_index("user")
     part = rows // peers
     start = pl.multiple_of(me * part, part)
-    out_ref[0:part, :] = v_ref[pl.ds(start, part), :]
-    out_ref[part : 2 * part, :] = dv_ref[pl.ds(start, part), :]
     time_ref[0:steps, :] = w_ref[...].astype(F32)
     time_ref[steps:, :] = dw_ref[...].astype(F32)
     piece = 2 * steps // peers
@@ -61,7 +59,7 @@
     row, lane = iota((8, LANES), 0), iota((8, LANES), 1)
     wanted = row * slots + lane % slots
     table = jnp.full((8, LANES), -1, jnp.int32)
-    count = count_ref[0, 0]
+    count = count_ref[0]
     for n in range(slot_ref.shape[2]):
         hit = (wanted == slot_ref[0, 0, n]) & (n < count)
         table = jnp.where(hit, item_ref[0, 0, n], table)
@@ -69,7 +67,9 @@
     for j in range(peers):
         for s in range(slots):
             table = jnp.where((row == peers) & (entry == j * slots + s), send_ref[0, 0, j, s], table)
-    out_ref[2 * part :, :] = jnp.concatenate([time_rows, table.astype(F32)], axis=0).astype(BF16)
+    last = jnp.concatenate([time_rows, table.astype(F32)], axis=0).astype(BF16)
+    whole = jnp.concatenate([v_ref[pl.ds(start, part), :], dv_ref[pl.ds(start, part), :], last], axis=0)
+    out_ref[...] = jnp.broadcast_to(whole[None], out_ref.shape)
 
 
 def gram_kernel(u_ref, du_ref, out_ref):
@@ -79,7 +79,7 @@
         out_ref[g] = dot_tn(jnp.concatenate([u, du_ref[at, :]], axis=1), u)
         return carry
 
-    lax.fori_loop(0, out_ref.shape[0], one, 0)
+    lax.fori_loop(0, out_ref.shape[0], one, 0, unroll=4)
 
 
 def weighted(table, wt, ww):
@@ -182,7 +182,7 @@
         a, b = carry
         return a + d * y + s * z, b + s * y
 
-    a, b = lax.fori_loop(0, blocks, item_terms, (zero, zero), unroll=2)
+    a, b = lax.fori_loop(0, blocks, item_terms, (zero, zero), unroll=4)
     left = jnp.concatenate([v_ref[...], dv_ref[...]], axis=1)
     item_rows = OBS_WEIGHT * dot_split(left, jnp.concatenate([a, b], axis=0))
 
@@ -213,11 +213,23 @@
         out_ref[at, :] = OBS_WEIGHT * term + LAMBDA_USER * du.astype(F32)
         return carry
 
-    lax.fori_loop(0, out_ref.shape[0] // UB, one, 0)
+    lax.fori_loop(0, out_ref.shape[0] // UB, one, 0, unroll=4)
+
+
+def finish_kernel(rows, *refs):
+    item_ref, time_ref = refs[-2:]
+    item_ref[...] = functools.reduce(jnp.add, [ref[:rows, :] for ref in refs[:-2]])
+    time_ref[...] = functools.reduce(jnp.add, [ref[rows:, :] for ref in refs[:-2]])
 
 
 def shape(dims, dtype=F32):
     return jax.ShapeDtypeStruct(dims, dtype)
+
+
+def placed(small):
+    if not small:
+        return shape, lambda *arrays: arrays
+    return pltpu.VMEM, lambda *arrays: [pltpu.with_memory_space_constraint(x, pltpu.VMEM) for x in arrays]
 
 
 def body(user_factor, user_tangent, item_factor, item_tangent, time_factor, time_tangent, send_list, tile_slot, tile_item, tile_count):
@@ -227,47 +239,52 @@
     blocks = user_factor.shape[0] // UB
     dims = (tm, peers, tiles, steps, rows)
     chunks = tm * steps // LANES
+    near, held = placed(chunks == 1 and tiles <= 2)
     height = 2 * rows // peers + 2 * steps // peers + 8
     packed = pl.pallas_call(
         functools.partial(pack_kernel, dims),
-        out_shape=shape((height, R), BF16),
+        out_shape=near((tm * peers, height, R), BF16),
         in_specs=[VM] * 4 + [SM] * 4,
         out_specs=VM,
         scratch_shapes=[pltpu.VMEM((2 * steps, R), F32)],
         name="pack",
-    )(item_factor, item_tangent, time_factor, time_tangent, send_list, tile_slot, tile_item, tile_count)
+    )(item_factor, item_tangent, time_factor, time_tangent, send_list, tile_slot, tile_item, tile_count.reshape(1))
     grams = pl.pallas_call(
-        gram_kernel, out_shape=shape((blocks, 2 * R, R)), in_specs=[VM] * 2, out_specs=VM, name="grams"
+        gram_kernel, out_shape=near((blocks, 2 * R, R), F32), in_specs=[VM] * 2, out_specs=VM, name="grams"
     )(user_factor, user_tangent)
     got = lax.all_to_all(
-        jnp.broadcast_to(packed[None], (tm * peers, height, R)), ("tm", "user"), split_axis=0, concat_axis=0, tiled=True
+        packed, ("tm", "user"), split_axis=0, concat_axis=0, tiled=True
     )
     partial, wt, ww, gh, counts, _ = pl.pallas_call(
         functools.partial(partial_kernel, dims),
         out_shape=(
-            shape((rows + steps, R)),
-            shape((chunks, 2 * R, LANES)),
-            shape((chunks, 2 * LANES, R), BF16),
-            shape((tiles, 2 * R, R)),
-            shape((chunks, blocks * tiles, LANES)),
-            shape((blocks * tiles, LANES)),
+            near((rows + steps, R), F32),
+            near((chunks, 2 * R, LANES), F32),
+            near((chunks, 2 * LANES, R), BF16),
+            near((tiles, 2 * R, R), F32),
+            near((chunks, blocks * tiles, LANES), F32),
+            near((blocks * tiles, LANES), F32),
         ),
         in_specs=[VM] * 6,
         out_specs=(VM,) * 6,
         name="partials",
-    )(got, grams, item_factor, item_tangent, time_factor, time_tangent)
-    step = 1
-    while step < peers:
-        partial = partial + lax.ppermute(partial, "user", [(i, i ^ step) for i in range(peers)])
-        step *= 2
+    )(*held(got, grams), item_factor, item_tangent, time_factor, time_tangent)
+    others = [lax.ppermute(partial, "user", [(i, (i + d) % peers) for i in range(peers)]) for d in range(1, peers)]
     user_hvp = pl.pallas_call(
         functools.partial(user_kernel, dims),
         out_shape=shape(user_factor.shape),
         in_specs=[VM] * 6,
         out_specs=VM,
         name="user_rows",
-    )(user_factor, user_tangent, wt, ww, gh, counts)
-    return (user_hvp, partial[:rows], partial[rows:])
+    )(user_factor, user_tangent, *held(wt, ww, gh, counts))
+    item_hvp, time_hvp = pl.pallas_call(
+        functools.partial(finish_kernel, rows),
+        out_shape=(shape((rows, R)), shape((steps, R))),
+        in_specs=[VM] * peers,
+        out_specs=(VM, VM),
+        name="finish",
+    )(*held(partial), *held(*others))
+    return (user_hvp, item_hvp, time_hvp)
 
 
 def solution(mesh):

time: 43.8 us -> 36.4 us (0.83); the launches traced: 42.9 us -> 35.9 us
  Pallas kernels: 20.9 us -> 14.2 us
  local copies, waits for them, and re-layouts: 3.47 us -> 0 us
  waiting for transfers between devices: 7.7 us -> 10.1 us
  starting transfers between devices: 8.72 us -> 10.4 us
  other arithmetic: 0.79 us -> 0 us
    pallas_call x3 -> x4, Pallas kernels: 12.3 us -> 7.77 us  [the longest x1 3.24 us: body(): pl.pallas_call(functools.partial(partial_kernel, dims), out_shape=(near((...]
    all_to_all x1, waiting for transfers between devices: 6.62 us -> 10.1 us  [body(): lax.all_to_all(packed, ('tm', 'user'), split_axis=0, concat_axis=0, tiled...]
    pallas_call x1, Pallas kernels: 8.63 us -> 6.41 us  [body(): pl.pallas_call(functools.partial(user_kernel, dims), out_shape=shape(user...]
    ppermute x2 -> x3, starting transfers between devices: 1.64 us -> 3.31 us  [body(): lax.ppermute(partial, 'user', [(i, (i + d) % peers) for i in range(peers)])]
    broadcast_in_dim x1 -> x0, local copies, waits for them, and re-layouts: 1.5 us -> none  [body(): jnp.broadcast_to(packed[None], (tm * peers, height, R))]
    slice x2 -> x0, local copies, waits for them, and re-layouts: 1.22 us -> none  [body(): return (user_hvp, partial[:rows], partial[rows:])]
    ppermute x2 -> x3, waiting for transfers between devices: 1.08 us -> 0.01 us  [body(): lax.ppermute(partial, 'user', [(i, (i + d) % peers) for i in range(peers)])]
    add x2 -> x0, other arithmetic: 0.79 us -> none  [body(): partial + lax.ppermute(partial, 'user', [(i, i ^ step) for i in range(pee...]
  transfers between devices with their start and end apart: 3 -> 4, of which waited for: 2 -> 1; matrix products, arithmetic and copies ran while one was open for 0% -> 0% of each run, Pallas kernels for 33% -> 24%
where the time goes in v2:
time: 36.4 us; the launch traced here: 35.9 us
  Pallas kernels  14.2 us (39%)
  starting transfers between devices  10.4 us (29%)
  waiting for transfers between devices  10.1 us (28%)
  between operations  1.3 us (4%)
    all_to_all x1, waiting for transfers between devices, body(): lax.all_to_all(packed, ('tm', 'user'), split_axis=0, concat_axis=0, tiled...  10.1 us
    all_to_all x1, starting transfers between devices, body(): lax.all_to_all(packed, ('tm', 'user'), split_axis=0, concat_axis=0, tiled...  7.08 us
    pallas_call x1, Pallas kernels, body(): pl.pallas_call(functools.partial(user_kernel, dims), out_shape=shape(user...  6.41 us
    ppermute x3, starting transfers between devices, body(): lax.ppermute(partial, 'user', [(i, (i + d) % peers) for i in range(peers)])  3.31 us
    pallas_call x1, Pallas kernels, body(): pl.pallas_call(functools.partial(partial_kernel, dims), out_shape=(near((...  3.24 us
    pallas_call x1, Pallas kernels, body(): pl.pallas_call(gram_kernel, out_shape=near((blocks, 2 * R, R), F32), in_s...  2.24 us
    pallas_call x1, Pallas kernels, body(): pl.pallas_call(functools.partial(pack_kernel, dims), out_shape=near((tm *...  1.66 us
  transfers between devices with their start and end apart: 4, of which 1 were waited for; matrix products, arithmetic and copies ran while one was open for 0% of the time, Pallas kernels for 24%

profile of v2, /device:TPU:1, one launch (start us, length us, event | category | flops | bytes accessed | tf_op | source)
XLA Modules:
  0.0 35.9 jit_solution(15691785889654251865)
XLA Ops:
  1.3 1.7 %pack.1 = bf16[32,48,128]{2,1,0:T(8,128)(2,1)} custom-call(bf16[64,128]{1,0:T(8,128)(2,1)} %v_ref.3, bf16[64,128]{1,0:T(8,128)(2,1)} %dv_ref.3, bf16[16,128]{1,0:T(8,128)(2,1)} %w_ref.3, bf16[16,128]{1,0:T(8,128)(2,1)} %dw_ref.3, s32[1,1,4,4]{3,2,1,0:T(4,128)} %send_ref.1, s32[1,1,16]{2,1,0:T(1,128)} %slot_ref.1, s32[1,1,16]{2,1,0:T(1,128)} %item_ref.1, ...), custom_call_target="tpu_custom_call" | custom-call | tf_op jit(solution)/shard_map/pack/pallas_call | solution.py:244
  2.9 7.1 %all-to-all-start = ((bf16[32,48,128]{2,1,0:T(8,128)(2,1)}), bf16[32,48,128]{2,1,0:T(8,128)(2,1)S(1)}, u32[]{:S(2)}, u32[]{:S(2)}) async-start(bf16[32,48,128]{2,1,0:T(8,128)(2,1)} %pack.1), calls=%async_computation | async-start | bytes 786432 | tf_op jit(solution)/shard_map/all_to_all | solution.py:255
  10.0 2.2 %grams.1.gram_ref = f32[16,256,128]{2,1,0:T(8,128)S(1)} custom-call(bf16[2048,128]{1,0:T(8,128)(2,1)} %u_ref.3, bf16[2048,128]{1,0:T(8,128)(2,1)} %du_ref.3), custom_call_target="tpu_custom_call" | custom-call | tf_op jit(solution)/shard_map/grams/pallas_call | solution.py:252
  12.3 10.1 %all-to-all-done.got_ref = bf16[32,48,128]{2,1,0:T(8,128)(2,1)S(1)} async-done(((bf16[32,48,128]{2,1,0:T(8,128)(2,1)}), bf16[32,48,128]{2,1,0:T(8,128)(2,1)S(1)}, u32[]{:S(2)}, u32[]{:S(2)}) %all-to-all-start) | async-done | bytes 393248 | tf_op jit(solution)/shard_map/all_to_all | solution.py:255
  22.3 3.2 %partials.1 = (f32[80,128]{1,0:T(8,128)S(1)}, f32[1,256,128]{2,1,0:T(8,128)S(1)}, bf16[1,256,128]{2,1,0:T(8,128)(2,1)S(1)}, f32[2,256,128]{2,1,0:T(8,128)S(1)}, ...) custom-call(bf16[32,48,128]{2,1,0:T(8,128)(2,1)S(1)} %all-to-all-done.got_ref, f32[16,256,128]{2,1,0:T(8,128)S(1)} %grams.1.gram_ref, ...), custom_call_target="tpu_custom_call" | custom-call | tf_op jit(solution)/shard_map/partials/pallas_call | solution.py:258
  25.6 1.2 %collective-permute-start.2 = (f32[80,128]{1,0:T(8,128)S(1)}, f32[80,128]{1,0:T(8,128)S(1)}, u32[]{:S(2)}, u32[]{:S(2)}) collective-permute-start(f32[80,128]{1,0:T(8,128)S(1)} %get-tuple-element.14.refs_0_), channel_id=1, source_target_pairs={{0,3},{1,0},{2,1},{3,2},{4,7},{5,4},{6,5},{7,6},{8,11},{9,8},{10,9... | collective-permute-start | bytes 122888 | tf_op jit(solution)/shard_map/ppermute | solution.py:272
  26.8 0.1 collective-permute-start.1
  26.9 2.0 %collective-permute-start = (f32[80,128]{1,0:T(8,128)S(1)}, f32[80,128]{1,0:T(8,128)S(1)}, u32[]{:S(2)}, u32[]{:S(2)}) collective-permute-start(f32[80,128]{1,0:T(8,128)S(1)} %get-tuple-element.14.refs_0_), channel_id=1, source_target_pairs={{0,1},{1,2},{2,3},{3,0},{4,5},{5,6},{6,7},{7,4},{8,9},{9,10},{10,1... | collective-permute-start | bytes 122888 | tf_op jit(solution)/shard_map/ppermute | solution.py:272
  28.9 6.4 %user_rows.1 = f32[2048,128]{1,0:T(8,128)} custom-call(bf16[2048,128]{1,0:T(8,128)(2,1)} %u_ref.3, bf16[2048,128]{1,0:T(8,128)(2,1)} %du_ref.3, f32[1,256,128]{2,1,0:T(8,128)S(1)} %get-tuple-element.10.wt_ref, bf16[1,256,128]{2,1,0:T(8,128)(2,1)S(1)} %get-tuple-element.11.ww_ref, f32[2,256,128]{2,1,0:T(8,128)S(1)} %get-tuple-element.12.gh_ref, ...), custom_call_target="tpu_custom_call" | custom-call | tf_op jit(solution)/shard_map/user_rows/pallas_call | solution.py:273
  35.3 0.0 collective-permute-done.2.refs_3_
  35.3 0.0 collective-permute-done.1.refs_2_
  35.3 0.0 collective-permute-done.refs_1_
  35.3 0.6 %finish.1 = (f32[64,128]{1,0:T(8,128)}, f32[16,128]{1,0:T(8,128)}) custom-call(f32[80,128]{1,0:T(8,128)S(1)} %get-tuple-element.14.refs_0_, f32[80,128]{1,0:T(8,128)S(1)} %collective-permute-done.refs_1_, f32[80,128]{1,0:T(8,128)S(1)} %collective-permute-done.1.refs_2_, f32[80,128]{1,0:T(8,128)S(1)} %collective-permute-done.2.refs_3_), custom_call_target="tpu_custom_call" | custom-call | tf_op jit(solution)/shard_map/finish/pallas_call | solution.py:280
Async XLA Ops:
  2.9 19.4 %all-to-all-start = ((bf16[32,48,128]{2,1,0:T(8,128)(2,1)}), bf16[32,48,128]{2,1,0:T(8,128)(2,1)S(1)}, u32[]{:S(2)}, u32[]{:S(2)}) async-start(bf16[32,48,128]{2,1,0:T(8,128)(2,1)} %pack.1), calls=%async_computation | async-start | bytes 786432 | tf_op jit(solution)/shard_map/all_to_all | solution.py:255
  25.6 9.7 %collective-permute-start.2 = (f32[80,128]{1,0:T(8,128)S(1)}, f32[80,128]{1,0:T(8,128)S(1)}, u32[]{:S(2)}, u32[]{:S(2)}) collective-permute-start(f32[80,128]{1,0:T(8,128)S(1)} %get-tuple-element.14.refs_0_), channel_id=1, source_target_pairs={{0,3},{1,0},{2,1},{3,2},{4,7},{5,4},{6,5},{7,6},{8,11},{9,8},{10,9... | collective-permute-start | bytes 122888 | tf_op jit(solution)/shard_map/ppermute | solution.py:272
  26.8 8.5 %collective-permute-start.1 = (f32[80,128]{1,0:T(8,128)S(1)}, f32[80,128]{1,0:T(8,128)S(1)}, u32[]{:S(2)}, u32[]{:S(2)}) collective-permute-start(f32[80,128]{1,0:T(8,128)S(1)} %get-tuple-element.14.refs_0_), channel_id=1, source_target_pairs={{0,2},{1,3},{2,0},{3,1},{4,6},{5,7},{6,4},{7,5},{8,10},{9,11},{10,... | collective-permute-start | bytes 122888 | tf_op jit(solution)/shard_map/ppermute | solution.py:272
  26.9 8.4 %collective-permute-start = (f32[80,128]{1,0:T(8,128)S(1)}, f32[80,128]{1,0:T(8,128)S(1)}, u32[]{:S(2)}, u32[]{:S(2)}) collective-permute-start(f32[80,128]{1,0:T(8,128)S(1)} %get-tuple-element.14.refs_0_), channel_id=1, source_target_pairs={{0,1},{1,2},{2,3},{3,0},{4,5},{5,6},{6,7},{7,4},{8,9},{9,10},{10,1... | collective-permute-start | bytes 122888 | tf_op jit(solution)/shard_map/ppermute | solution.py:272

commit v3 on v2

--- a/solution.py
+++ b/solution.py
@@ -11,6 +11,7 @@
 UB = 128
 IT = 256
 LANES = 128
+SUB = 8
 
 OBS_WEIGHT = 0.03125
 LAMBDA_USER = 0.5
@@ -20,6 +21,7 @@
 F32 = jnp.float32
 BF16 = jnp.bfloat16
 VM = pl.BlockSpec(memory_space=pltpu.VMEM)
+HBM = pl.BlockSpec(memory_space=pltpu.HBM)
 SM = pl.BlockSpec(memory_space=pltpu.SMEM)
 
 
@@ -73,23 +75,50 @@
 
 
 def gram_kernel(u_ref, du_ref, out_ref):
-    def one(g, carry):
-        at = pl.ds(pl.multiple_of(g * UB, UB), UB)
-        u = u_ref[at, :]
-        out_ref[g] = dot_tn(jnp.concatenate([u, du_ref[at, :]], axis=1), u)
+    blocks = u_ref.shape[0] // UB
+    groups = R // SUB
+
+    def pair(i, carry):
+        sides = []
+        for g in (2 * i, 2 * i + 1):
+            at = pl.ds(pl.multiple_of(g * UB, UB), UB)
+            u = u_ref[at, :]
+            gram = dot_tn(jnp.concatenate([u, du_ref[at, :]], axis=1), u)
+            sides.append(jnp.concatenate([gram[:R], gram[R:]], axis=1).reshape(groups, SUB, 2 * R))
+        high, low = halves(jnp.concatenate(sides, axis=1))
+        at = pl.multiple_of(i * 2 * SUB, 2 * SUB)
+        out_ref[:, pl.ds(at, 2 * SUB), :] = high
+        out_ref[:, pl.ds(at + blocks * SUB, 2 * SUB), :] = low
         return carry
 
-    lax.fori_loop(0, out_ref.shape[0], one, 0, unroll=4)
-
-
-def weighted(table, wt, ww):
-    high, low = halves(wt * table)
-    return dot_nn(jnp.concatenate([high, low], axis=1), ww)
-
-
-def partial_kernel(dims, got_ref, gram_ref, v_ref, dv_ref, w_ref, dw_ref, out_ref, wt_ref, ww_ref, gh_ref, c_ref, own_ref):
+    lax.fori_loop(0, blocks // 2, pair, 0, unroll=2)
+
+
+def dot_nt(left, right):
+    return lax.dot_general(left, right, (((1,), (1,)), ((), ())), preferred_element_type=F32)
+
+
+def count_rows(left, right, keep):
+    counts = dot_nt(left.astype(BF16), right.astype(BF16))
+    same = iota(counts.shape, 0) % SUB == iota(counts.shape, 1) % SUB
+    counts = jnp.where(same, counts, 0.0).astype(BF16)
+    return jnp.concatenate([counts, counts], axis=1) if keep else counts
+
+
+def time_grams(wt, w, out_ref, at, steps):
+    owner = iota((LANES, R), 0) // steps
+    zero = jnp.zeros((LANES, R), BF16)
+    for a in range(0, LANES // steps, 2):
+        right = jnp.concatenate([jnp.where(owner == a + i, w, zero) for i in range(2)], axis=1)
+        both = dot_nn(wt, right)
+        out_ref[at + a] = both[:, :R]
+        out_ref[at + a + 1] = both[:, R:]
+
+
+def partial_kernel(dims, got_ref, gram_ref, v_ref, dv_ref, w_ref, dw_ref, out_ref, wt_ref, ww_ref, gh_ref, entry_ref, left_ref, grams_ref):
     tm, peers, tiles, steps, rows = dims
-    blocks = gram_ref.shape[0]
+    groups, depth = gram_ref.shape[:2]
+    blocks = depth // (2 * SUB)
     part = rows // peers
     piece = 2 * steps // peers
     entries = LANES // steps
@@ -97,12 +126,13 @@
     me_tm, me = lax.axis_index("tm"), lax.axis_index("user")
     lane, row8 = iota((8, LANES), 1), iota((8, LANES), 0)
     slots = steps // peers
-
-    owner = iota((LANES, LANES), 0) // steps
-    spread = (owner == iota((LANES, LANES), 1) // steps).astype(BF16)
+    my_tile = me_tm * rows // IT
+
     coeff_rows = me_tm * steps + iota((steps, LANES), 0)
     penalty = jnp.zeros((steps, R), F32)
     total_steps = tm * steps
+    item_height = entries * SUB
+    own_counts = jnp.zeros((tiles * SUB, blocks * SUB), BF16)
     for chunk in range(chunks):
         base = chunk * entries
         pieces = []
@@ -120,17 +150,20 @@
         half = peers // 2
         w = jnp.concatenate([pieces[a * peers + j] for a in range(entries) for j in range(half)], axis=0)
         dw = jnp.concatenate([pieces[a * peers + j] for a in range(entries) for j in range(half, peers)], axis=0)
-        ww = w.astype(BF16)
-        wt_ref[chunk] = jnp.concatenate([w, dw], axis=1).T
-        ww_ref[chunk] = jnp.concatenate([ww, ww], axis=0)
-        item = jnp.sum(found_m, axis=0, keepdims=True)
-        block = jnp.sum(found_g, axis=0, keepdims=True)
-        number = jnp.where(item < 0.0, -1.0, block * tiles + item).astype(jnp.int32)
-        hot = (iota((blocks * tiles, LANES), 0) == number).astype(BF16)
-        mine = (owner == me_tm - base).astype(BF16)
-        counts = dot_nn(hot, jnp.concatenate([spread, mine], axis=1))
-        c_ref[chunk] = counts[:, :LANES]
-        own_ref[...] = counts[:, LANES:] + (own_ref[...] if chunk else 0.0)
+        wt_ref[chunk] = jnp.concatenate([w, dw], axis=1).T.astype(BF16)
+        ww_ref[chunk] = w.astype(BF16)
+        time_grams(wt_ref[chunk], ww_ref[chunk], grams_ref, base, steps)
+        item = jnp.sum(found_m, axis=0, keepdims=True).astype(jnp.int32)
+        block = jnp.sum(found_g, axis=0, keepdims=True).astype(jnp.int32)
+        entry_ref[chunk, 0:1, :] = item
+        entry_ref[chunk, 1:2, :] = block
+        shape_left, shape_right = (item_height, LANES), (blocks * SUB, LANES)
+        right = block == iota(shape_right, 0) // SUB
+        left = (iota(shape_left, 1) // steps == iota(shape_left, 0) // SUB) & (item == my_tile)
+        left_ref[pl.ds(chunk * item_height, item_height), :] = count_rows(left, right, True)
+        shape_left = (tiles * SUB, LANES)
+        left = (iota(shape_left, 1) // steps == me_tm - base) & (item == iota(shape_left, 0) // SUB)
+        own_counts = own_counts + count_rows(left, right, False)
         column = chunk * LANES + iota((steps, LANES), 1)
         coeff = jnp.zeros((steps, LANES), F32)
         for shift, scale in ((-1, 1.0), (0, -2.0), (1, 1.0)):
@@ -140,6 +173,7 @@
             value = jnp.where(apart == 0, -2.0, jnp.where(jnp.abs(apart) == 1, 1.0, 0.0))
             coeff = coeff + jnp.where(inside, scale * value, 0.0)
         penalty = penalty + dot_nn(coeff.astype(BF16), dw.astype(BF16))
+    left_ref[pl.ds(chunks * item_height, tiles * SUB), :] = jnp.concatenate([own_counts, own_counts], axis=1)
 
     per_tile = IT // rows
 
@@ -156,64 +190,95 @@
 
     lax.fori_loop(0, tiles, item_grams, 0, unroll=tiles <= 2)
 
-    def time_terms(m, carry):
-        def add(g, total):
-            return total + own_ref[pl.ds(g * tiles + m, 1), :] * gram_ref[g]
-
-        total = lax.fori_loop(0, blocks, add, jnp.zeros((2 * R, R), F32), unroll=4)
-        s, d = total[:R], total[R:]
-        g_m, h_m = gh_ref[m, :R], gh_ref[m, R:]
-        q, r = carry
-        return q + d * g_m + s * h_m, r + s * g_m
-
-    zero = jnp.zeros((R, R), F32)
-    q, r = lax.fori_loop(0, tiles, time_terms, (zero, zero), unroll=tiles <= 2)
+    sides = ([], [], [], [])
+    for group in range(groups):
+        sums = dot_nn(left_ref[...], gram_ref[group])
+        s, d = sums[:, :R], sums[:, R:]
+        at = pl.ds(group * SUB, SUB)
+        below = pl.ds(R + group * SUB, SUB)
+        a_rows = b_rows = q_rows = r_rows = jnp.zeros((SUB, R), F32)
+        for a in range(tm):
+            here = slice(a * SUB, (a + 1) * SUB)
+            y, z = grams_ref[a, at, :], grams_ref[a, below, :]
+            a_rows = a_rows + d[here] * y + s[here] * z
+            b_rows = b_rows + s[here] * y
+        for m in range(tiles):
+            here = slice((tm + m) * SUB, (tm + m + 1) * SUB)
+            g_m, h_m = gh_ref[m, at, :], gh_ref[m, below, :]
+            q_rows = q_rows + d[here] * g_m + s[here] * h_m
+            r_rows = r_rows + s[here] * g_m
+        for side, value in zip(sides, (a_rows, b_rows, q_rows, r_rows)):
+            side.append(value)
+    left = jnp.concatenate([v_ref[...], dv_ref[...]], axis=1)
+    item_rows = OBS_WEIGHT * dot_split(left, jnp.concatenate(sides[0] + sides[1], axis=0))
     left = jnp.concatenate([w_ref[...], dw_ref[...]], axis=1)
-    time_rows = OBS_WEIGHT * dot_split(left, jnp.concatenate([q, r], axis=0))
-
-    my_tile = me_tm * rows // IT
-
-    def item_terms(g, carry):
-        s, d = gram_ref[g, :R], gram_ref[g, R:]
-        both = jnp.zeros((2 * R, R), F32)
-        for chunk in range(chunks):
-            both = both + weighted(c_ref[chunk, pl.ds(g * tiles + my_tile, 1), :], wt_ref[chunk], ww_ref[chunk])
-        y, z = both[:R], both[R:]
-        a, b = carry
-        return a + d * y + s * z, b + s * y
-
-    a, b = lax.fori_loop(0, blocks, item_terms, (zero, zero), unroll=4)
-    left = jnp.concatenate([v_ref[...], dv_ref[...]], axis=1)
-    item_rows = OBS_WEIGHT * dot_split(left, jnp.concatenate([a, b], axis=0))
-
+    time_rows = OBS_WEIGHT * dot_split(left, jnp.concatenate(sides[2] + sides[3], axis=0))
     first = jnp.where(me == 0, 1.0, 0.0)
     out_ref[:rows, :] = item_rows + (first * LAMBDA_ITEM) * dv_ref[...].astype(F32)
     out_ref[rows:, :] = time_rows + (first * LAMBDA_TIME) * penalty
 
 
-def user_kernel(dims, u_ref, du_ref, wt_ref, ww_ref, gh_ref, c_ref, out_ref):
+def user_kernel(dims, u_hbm, du_hbm, wt_ref, ww_ref, gh_ref, entry_ref, out_hbm, u_ref, du_ref, out_ref, grams_ref, k_ref, in_sem, out_sem):
     tm, peers, tiles, steps, rows = dims
     chunks = wt_ref.shape[0]
-
-    def one(g, carry):
-        def add(m, total):
-            both = jnp.zeros((2 * R, R), F32)
-            for chunk in range(chunks):
-                both = both + weighted(c_ref[chunk, pl.ds(g * tiles + m, 1), :], wt_ref[chunk], ww_ref[chunk])
-            y, z = both[:R], both[R:]
-            g_m, h_m = gh_ref[m, :R], gh_ref[m, R:]
-            return total[0] + g_m * y, total[1] + g_m * z + h_m * y
-
-        zero = jnp.zeros((R, R), F32)
-        k_delta, k_factor = lax.fori_loop(0, tiles, add, (zero, zero), unroll=tiles <= 2)
-        at = pl.ds(pl.multiple_of(g * UB, UB), UB)
-        du = du_ref[at, :]
-        left = jnp.concatenate([du, u_ref[at, :]], axis=1)
-        term = dot_split(left, jnp.concatenate([k_delta, k_factor], axis=0))
-        out_ref[at, :] = OBS_WEIGHT * term + LAMBDA_USER * du.astype(F32)
-        return carry
-
-    lax.fori_loop(0, out_ref.shape[0] // UB, one, 0, unroll=4)
+    entries = LANES // steps
+    blocks, groups = k_ref.shape[0], R // SUB
+    loads = [
+        pltpu.make_async_copy(u_hbm, u_ref, in_sem.at[0]),
+        pltpu.make_async_copy(du_hbm, du_ref, in_sem.at[1]),
+    ]
+    for load in loads:
+        load.start()
+
+    width = LANES // (entries * SUB)
+
+    def add(chunk, first, fresh):
+        item, block = entry_ref[chunk, 0:1, :], entry_ref[chunk, 1:2, :]
+        left = block == iota((blocks * SUB, LANES), 0) // SUB
+        shape_right = (entries * width * SUB, LANES)
+        place = iota(shape_right, 0) // SUB
+        right = (iota(shape_right, 1) // steps == place // width) & (item == first + place % width)
+        counts = count_rows(left, right, True)
+        for group in range(groups):
+            at = pl.ds(group * SUB, SUB)
+            below = pl.ds(R + group * SUB, SUB)
+            stack = []
+            for a in range(entries):
+                y, z = grams_ref[a, at, :], grams_ref[a, below, :]
+                for m in range(width):
+                    g_m, h_m = gh_ref[first + m, at, :], gh_ref[first + m, below, :]
+                    stack.append(jnp.concatenate([g_m * y, g_m * z + h_m * y], axis=1))
+            high, low = halves(jnp.concatenate(stack, axis=0))
+            value = dot_nn(counts, jnp.concatenate([high, low], axis=0)).reshape(blocks, SUB, 2 * R)
+            k_ref[:, at, :] = value if fresh else k_ref[:, at, :] + value
+
+    for chunk in range(chunks):
+        time_grams(wt_ref[chunk], ww_ref[chunk], grams_ref, 0, steps)
+        add(chunk, 0, chunk == 0)
+
+        def rest(i, carry):
+            add(chunk, i * width, False)
+            return carry
+
+        lax.fori_loop(1, tiles // width, rest, 0)
+
+    for load in loads:
+        load.wait()
+    stores = []
+    per_store = blocks // out_sem.shape[0]
+    for number in range(out_sem.shape[0]):
+        for g in range(number * per_store, (number + 1) * per_store):
+            at = pl.ds(g * UB, UB)
+            du = du_ref[at, :]
+            left = jnp.concatenate([du, u_ref[at, :]], axis=1)
+            term = dot_split(left, jnp.concatenate([k_ref[g, :, :R], k_ref[g, :, R:]], axis=0))
+            out_ref[at, :] = OBS_WEIGHT * term + LAMBDA_USER * du.astype(F32)
+        at = pl.ds(number * per_store * UB, per_store * UB)
+        store = pltpu.make_async_copy(out_ref.at[at, :], out_hbm.at[at, :], out_sem.at[number])
+        store.start()
+        stores.append(store)
+    for store in stores:
+        store.wait()
 
 
 def finish_kernel(rows, *refs):
@@ -249,34 +314,51 @@
         scratch_shapes=[pltpu.VMEM((2 * steps, R), F32)],
         name="pack",
     )(item_factor, item_tangent, time_factor, time_tangent, send_list, tile_slot, tile_item, tile_count.reshape(1))
+    groups = R // SUB
     grams = pl.pallas_call(
-        gram_kernel, out_shape=near((blocks, 2 * R, R), F32), in_specs=[VM] * 2, out_specs=VM, name="grams"
+        gram_kernel,
+        out_shape=near((groups, 2 * SUB * blocks, 2 * R), BF16),
+        in_specs=[VM] * 2,
+        out_specs=VM,
+        name="grams",
     )(user_factor, user_tangent)
     got = lax.all_to_all(
         packed, ("tm", "user"), split_axis=0, concat_axis=0, tiled=True
     )
-    partial, wt, ww, gh, counts, _ = pl.pallas_call(
+    partial, wt, ww, gh, listed = pl.pallas_call(
         functools.partial(partial_kernel, dims),
         out_shape=(
             near((rows + steps, R), F32),
-            near((chunks, 2 * R, LANES), F32),
-            near((chunks, 2 * LANES, R), BF16),
+            near((chunks, 2 * R, LANES), BF16),
+            near((chunks, LANES, R), BF16),
             near((tiles, 2 * R, R), F32),
-            near((chunks, blocks * tiles, LANES), F32),
-            near((blocks * tiles, LANES), F32),
+            near((chunks, 8, LANES), jnp.int32),
         ),
         in_specs=[VM] * 6,
-        out_specs=(VM,) * 6,
+        out_specs=(VM,) * 5,
+        scratch_shapes=[
+            pltpu.VMEM(((tm + tiles) * SUB, 2 * SUB * blocks), BF16),
+            pltpu.VMEM((tm, 2 * R, R), F32),
+        ],
         name="partials",
     )(*held(got, grams), item_factor, item_tangent, time_factor, time_tangent)
     others = [lax.ppermute(partial, "user", [(i, (i + d) % peers) for i in range(peers)]) for d in range(1, peers)]
     user_hvp = pl.pallas_call(
         functools.partial(user_kernel, dims),
         out_shape=shape(user_factor.shape),
-        in_specs=[VM] * 6,
-        out_specs=VM,
+        in_specs=[HBM] * 2 + [VM] * 4,
+        out_specs=HBM,
+        scratch_shapes=[
+            pltpu.VMEM(user_factor.shape, BF16),
+            pltpu.VMEM(user_factor.shape, BF16),
+            pltpu.VMEM(user_factor.shape, F32),
+            pltpu.VMEM((LANES // steps, 2 * R, R), F32),
+            pltpu.VMEM((blocks, R, 2 * R), F32),
+            pltpu.SemaphoreType.DMA((2,)),
+            pltpu.SemaphoreType.DMA((4,)),
+        ],
         name="user_rows",
-    )(user_factor, user_tangent, *held(wt, ww, gh, counts))
+    )(user_factor, user_tangent, *held(wt, ww, gh, listed))
     item_hvp, time_hvp = pl.pallas_call(
         functools.partial(finish_kernel, rows),
         out_shape=(shape((rows, R)), shape((steps, R))),

time: 36.4 us -> 31.7 us (0.87)
  Pallas kernels: 14.2 us -> 9.46 us
    pallas_call x1, Pallas kernels: 6.41 us -> 3.15 us  [body(): pl.pallas_call(functools.partial(user_kernel, dims), out_shape=shape(user...]
    pallas_call x1, Pallas kernels: 3.24 us -> 1.72 us  [body(): pl.pallas_call(functools.partial(partial_kernel, dims), out_shape=(near((...]
  transfers between devices with their start and end apart: 4 -> 4, of which waited for: 1 -> 1; matrix products, arithmetic and copies ran while one was open for 0% -> 0% of each run, Pallas kernels for 24% -> 17%
where the time goes in v3:
time: 31.7 us; the launch traced here: 31.2 us
  starting transfers between devices  10.4 us (33%)
  waiting for transfers between devices  9.99 us (32%)
  Pallas kernels  9.46 us (30%)
  between operations  1.33 us (4%)
    all_to_all x1, waiting for transfers between devices, body(): lax.all_to_all(packed, ('tm', 'user'), split_axis=0, concat_axis=0, tiled...  9.99 us
    all_to_all x1, starting transfers between devices, body(): lax.all_to_all(packed, ('tm', 'user'), split_axis=0, concat_axis=0, tiled...  7.08 us
    ppermute x3, starting transfers between devices, body(): lax.ppermute(partial, 'user', [(i, (i + d) % peers) for i in range(peers)])  3.37 us
    pallas_call x1, Pallas kernels, body(): pl.pallas_call(functools.partial(user_kernel, dims), out_shape=shape(user...  3.15 us
    pallas_call x1, Pallas kernels, body(): pl.pallas_call(gram_kernel, out_shape=near((groups, 2 * SUB * blocks, 2 *...  2.3 us
    pallas_call x1, Pallas kernels, body(): pl.pallas_call(functools.partial(partial_kernel, dims), out_shape=(near((...  1.72 us
    pallas_call x1, Pallas kernels, body(): pl.pallas_call(functools.partial(pack_kernel, dims), out_shape=near((tm *...  1.66 us
  transfers between devices with their start and end apart: 4, of which 1 were waited for; matrix products, arithmetic and copies ran while one was open for 0% of the time, Pallas kernels for 17%

profile of v3, /device:TPU:1, one launch (start us, length us, event | category | flops | bytes accessed | tf_op | source)
XLA Modules:
  0.0 31.2 jit_solution(501368867159189830)
XLA Ops:
  1.3 1.7 %pack.1 = bf16[32,48,128]{2,1,0:T(8,128)(2,1)} custom-call(bf16[64,128]{1,0:T(8,128)(2,1)} %v_ref.3, bf16[64,128]{1,0:T(8,128)(2,1)} %dv_ref.3, bf16[16,128]{1,0:T(8,128)(2,1)} %w_ref.3, bf16[16,128]{1,0:T(8,128)(2,1)} %dw_ref.3, s32[1,1,4,4]{3,2,1,0:T(4,128)} %send_ref.1, s32[1,1,16]{2,1,0:T(1,128)} %slot_ref.1, s32[1,1,16]{2,1,0:T(1,128)} %item_ref.1, ...), custom_call_target="tpu_custom_call" | custom-call | tf_op jit(solution)/shard_map/pack/pallas_call | solution.py:309
  2.9 7.1 %all-to-all-start = ((bf16[32,48,128]{2,1,0:T(8,128)(2,1)}), bf16[32,48,128]{2,1,0:T(8,128)(2,1)S(1)}, u32[]{:S(2)}, u32[]{:S(2)}) async-start(bf16[32,48,128]{2,1,0:T(8,128)(2,1)} %pack.1), calls=%async_computation | async-start | bytes 786432 | tf_op jit(solution)/shard_map/all_to_all | solution.py:325
  10.0 2.3 %grams.1.gram_ref = bf16[16,256,256]{2,1,0:T(8,128)(2,1)S(1)} custom-call(bf16[2048,128]{1,0:T(8,128)(2,1)} %u_hbm.1, bf16[2048,128]{1,0:T(8,128)(2,1)} %du_hbm.1), custom_call_target="tpu_custom_call" | custom-call | tf_op jit(solution)/shard_map/grams/pallas_call | solution.py:318
  12.3 10.0 %all-to-all-done.got_ref = bf16[32,48,128]{2,1,0:T(8,128)(2,1)S(1)} async-done(((bf16[32,48,128]{2,1,0:T(8,128)(2,1)}), bf16[32,48,128]{2,1,0:T(8,128)(2,1)S(1)}, u32[]{:S(2)}, u32[]{:S(2)}) %all-to-all-start) | async-done | bytes 393248 | tf_op jit(solution)/shard_map/all_to_all | solution.py:325
  22.3 1.7 %partials.1 = (f32[80,128]{1,0:T(8,128)S(1)}, bf16[1,256,128]{2,1,0:T(8,128)(2,1)S(1)}, bf16[1,128,128]{2,1,0:T(8,128)(2,1)S(1)}, f32[2,256,128]{2,1,0:T(8,128)S(1)}, s32[1,8,128]{2,1,0:T(8,128)S(1)}) custom-call(bf16[32,48,128]{2,1,0:T(8,128)(2,1)S(1)} %all-to-all-done.got_ref, bf16[16,256,256]{2,1,0:T(8,128)(2,1)S(1)} %grams.1.gram_ref, ...), custom_call_target="tpu_custom_call" | custom-call | tf_op jit(solution)/shard_map/partials/pallas_call | solution.py:328
  24.1 1.3 %collective-permute-start.2 = (f32[80,128]{1,0:T(8,128)S(1)}, f32[80,128]{1,0:T(8,128)S(1)}, u32[]{:S(2)}, u32[]{:S(2)}) collective-permute-start(f32[80,128]{1,0:T(8,128)S(1)} %get-tuple-element.14.refs_0_), channel_id=1, source_target_pairs={{0,3},{1,0},{2,1},{3,2},{4,7},{5,4},{6,5},{7,6},{8,11},{9,8},{10,9... | collective-permute-start | bytes 122888 | tf_op jit(solution)/shard_map/ppermute | solution.py:345
  25.3 0.2 collective-permute-start.1
  25.5 1.9 %collective-permute-start = (f32[80,128]{1,0:T(8,128)S(1)}, f32[80,128]{1,0:T(8,128)S(1)}, u32[]{:S(2)}, u32[]{:S(2)}) collective-permute-start(f32[80,128]{1,0:T(8,128)S(1)} %get-tuple-element.14.refs_0_), channel_id=1, source_target_pairs={{0,1},{1,2},{2,3},{3,0},{4,5},{5,6},{6,7},{7,4},{8,9},{9,10},{10,1... | collective-permute-start | bytes 122888 | tf_op jit(solution)/shard_map/ppermute | solution.py:345
  27.4 3.1 %user_rows.1 = f32[2048,128]{1,0:T(8,128)} custom-call(bf16[2048,128]{1,0:T(8,128)(2,1)} %u_hbm.1, bf16[2048,128]{1,0:T(8,128)(2,1)} %du_hbm.1, bf16[1,256,128]{2,1,0:T(8,128)(2,1)S(1)} %get-tuple-element.10.wt_ref, bf16[1,128,128]{2,1,0:T(8,128)(2,1)S(1)} %get-tuple-element.11.ww_ref, f32[2,256,128]{2,1,0:T(8,128)S(1)} %get-tuple-element.12.gh_ref, ...), custom_call_target="tpu_custom_call" | custom-call | tf_op jit(solution)/shard_map/user_rows/pallas_call | solution.py:346
  30.6 0.0 collective-permute-done.2.refs_3_
  30.6 0.0 collective-permute-done.1.refs_2_
  30.6 0.0 collective-permute-done.refs_1_
  30.6 0.6 %finish.1 = (f32[64,128]{1,0:T(8,128)}, f32[16,128]{1,0:T(8,128)}) custom-call(f32[80,128]{1,0:T(8,128)S(1)} %get-tuple-element.14.refs_0_, f32[80,128]{1,0:T(8,128)S(1)} %collective-permute-done.refs_1_, f32[80,128]{1,0:T(8,128)S(1)} %collective-permute-done.1.refs_2_, f32[80,128]{1,0:T(8,128)S(1)} %collective-permute-done.2.refs_3_), custom_call_target="tpu_custom_call" | custom-call | tf_op jit(solution)/shard_map/finish/pallas_call | solution.py:362
Async XLA Ops:
  2.9 19.4 %all-to-all-start = ((bf16[32,48,128]{2,1,0:T(8,128)(2,1)}), bf16[32,48,128]{2,1,0:T(8,128)(2,1)S(1)}, u32[]{:S(2)}, u32[]{:S(2)}) async-start(bf16[32,48,128]{2,1,0:T(8,128)(2,1)} %pack.1), calls=%async_computation | async-start | bytes 786432 | tf_op jit(solution)/shard_map/all_to_all | solution.py:325
  24.1 6.5 %collective-permute-start.2 = (f32[80,128]{1,0:T(8,128)S(1)}, f32[80,128]{1,0:T(8,128)S(1)}, u32[]{:S(2)}, u32[]{:S(2)}) collective-permute-start(f32[80,128]{1,0:T(8,128)S(1)} %get-tuple-element.14.refs_0_), channel_id=1, source_target_pairs={{0,3},{1,0},{2,1},{3,2},{4,7},{5,4},{6,5},{7,6},{8,11},{9,8},{10,9... | collective-permute-start | bytes 122888 | tf_op jit(solution)/shard_map/ppermute | solution.py:345
  25.3 5.3 %collective-permute-start.1 = (f32[80,128]{1,0:T(8,128)S(1)}, f32[80,128]{1,0:T(8,128)S(1)}, u32[]{:S(2)}, u32[]{:S(2)}) collective-permute-start(f32[80,128]{1,0:T(8,128)S(1)} %get-tuple-element.14.refs_0_), channel_id=1, source_target_pairs={{0,2},{1,3},{2,0},{3,1},{4,6},{5,7},{6,4},{7,5},{8,10},{9,11},{10,... | collective-permute-start | bytes 122888 | tf_op jit(solution)/shard_map/ppermute | solution.py:345
  25.5 5.1 %collective-permute-start = (f32[80,128]{1,0:T(8,128)S(1)}, f32[80,128]{1,0:T(8,128)S(1)}, u32[]{:S(2)}, u32[]{:S(2)}) collective-permute-start(f32[80,128]{1,0:T(8,128)S(1)} %get-tuple-element.14.refs_0_), channel_id=1, source_target_pairs={{0,1},{1,2},{2,3},{3,0},{4,5},{5,6},{6,7},{7,4},{8,9},{9,10},{10,1... | collective-permute-start | bytes 122888 | tf_op jit(solution)/shard_map/ppermute | solution.py:345

commit v4 on v3

--- a/solution.py
+++ b/solution.py
@@ -61,7 +61,7 @@
     row, lane = iota((8, LANES), 0), iota((8, LANES), 1)
     wanted = row * slots + lane % slots
     table = jnp.full((8, LANES), -1, jnp.int32)
-    count = count_ref[0]
+    count = count_ref[0, 0]
     for n in range(slot_ref.shape[2]):
         hit = (wanted == slot_ref[0, 0, n]) & (n < count)
         table = jnp.where(hit, item_ref[0, 0, n], table)
@@ -115,7 +115,7 @@
         out_ref[at + a + 1] = both[:, R:]
 
 
-def partial_kernel(dims, got_ref, gram_ref, v_ref, dv_ref, w_ref, dw_ref, out_ref, wt_ref, ww_ref, gh_ref, entry_ref, left_ref, grams_ref):
+def partial_kernel(dims, got_ref, other_ref, gram_ref, v_ref, dv_ref, w_ref, dw_ref, out_ref, wt_ref, ww_ref, gh_ref, entry_ref, left_ref, grams_ref):
     tm, peers, tiles, steps, rows = dims
     groups, depth = gram_ref.shape[:2]
     blocks = depth // (2 * SUB)
@@ -126,6 +126,11 @@
     me_tm, me = lax.axis_index("tm"), lax.axis_index("user")
     lane, row8 = iota((8, LANES), 1), iota((8, LANES), 0)
     slots = steps // peers
+
+    def sent(a, j, first, last):
+        here = a * (peers // 2) + j // 2
+        return jnp.where(me % 2 == j % 2, got_ref[here, first:last, :], other_ref[here, first:last, :])
+
     my_tile = me_tm * rows // IT
 
     coeff_rows = me_tm * steps + iota((steps, LANES), 0)
@@ -140,7 +145,7 @@
         found_g = jnp.zeros((8, LANES), F32)
         for a in range(entries):
             for j in range(peers):
-                tile = got_ref[(base + a) * peers + j, 2 * part :, :].astype(F32)
+                tile = sent(base + a, j, 2 * part, 2 * part + 16).astype(F32)
                 pieces.append(tile[:piece])
                 mine = lane // steps == a
                 hit = mine & (row8 == me) & (lane // slots % peers == j)
@@ -180,7 +185,7 @@
     def item_grams(m, carry):
         def gathered(first):
             return jnp.concatenate(
-                [got_ref[(m * per_tile + a) * peers + j, first : first + part, :] for a in range(per_tile) for j in range(peers)],
+                [sent(m * per_tile + a, j, first, first + part) for a in range(per_tile) for j in range(peers)],
                 axis=0,
             )
 
@@ -308,12 +313,12 @@
     height = 2 * rows // peers + 2 * steps // peers + 8
     packed = pl.pallas_call(
         functools.partial(pack_kernel, dims),
-        out_shape=near((tm * peers, height, R), BF16),
+        out_shape=shape((tm * peers // 2, height, R), BF16),
         in_specs=[VM] * 4 + [SM] * 4,
         out_specs=VM,
         scratch_shapes=[pltpu.VMEM((2 * steps, R), F32)],
         name="pack",
-    )(item_factor, item_tangent, time_factor, time_tangent, send_list, tile_slot, tile_item, tile_count.reshape(1))
+    )(item_factor, item_tangent, time_factor, time_tangent, send_list, tile_slot, tile_item, tile_count)
     groups = R // SUB
     grams = pl.pallas_call(
         gram_kernel,
@@ -322,9 +327,12 @@
         out_specs=VM,
         name="grams",
     )(user_factor, user_tangent)
+    cores = [[i for i in range(tm * peers) if i % 2 == core] for core in range(2)]
     got = lax.all_to_all(
-        packed, ("tm", "user"), split_axis=0, concat_axis=0, tiled=True
+        packed, ("tm", "user"), split_axis=0, concat_axis=0, tiled=True, axis_index_groups=cores
     )
+    got, grams = lax.optimization_barrier((got, grams))
+    other = lax.ppermute(got, "user", [(i, i ^ 1) for i in range(peers)])
     partial, wt, ww, gh, listed = pl.pallas_call(
         functools.partial(partial_kernel, dims),
         out_shape=(
@@ -334,15 +342,15 @@
             near((tiles, 2 * R, R), F32),
             near((chunks, 8, LANES), jnp.int32),
         ),
-        in_specs=[VM] * 6,
+        in_specs=[VM] * 7,
         out_specs=(VM,) * 5,
         scratch_shapes=[
             pltpu.VMEM(((tm + tiles) * SUB, 2 * SUB * blocks), BF16),
             pltpu.VMEM((tm, 2 * R, R), F32),
         ],
         name="partials",
-    )(*held(got, grams), item_factor, item_tangent, time_factor, time_tangent)
-    others = [lax.ppermute(partial, "user", [(i, (i + d) % peers) for i in range(peers)]) for d in range(1, peers)]
+    )(*held(got, other, grams), item_factor, item_tangent, time_factor, time_tangent)
+    others = [lax.ppermute(partial, "user", [(i, i ^ d) for i in range(peers)]) for d in range(1, peers)]
     user_hvp = pl.pallas_call(
         functools.partial(user_kernel, dims),
         out_shape=shape(user_factor.shape),

time: 31.7 us -> 29.2 us (0.921)
  waiting for transfers between devices: 9.99 us -> 5.73 us
  starting transfers between devices: 10.4 us -> 12.2 us
    all_to_all x1, waiting for transfers between devices: 9.99 us -> 4.65 us  [body(): lax.all_to_all(packed, ('tm', 'user'), split_axis=0, concat_axis=0, tiled...]
    ppermute x3 -> x4, starting transfers between devices: 3.37 us -> 4.83 us  [the longest x1 2.63 us: body(): other = lax.ppermute(got, 'user', [(i, i ^ 1) for i in range(peers)])]
    ppermute x3 -> x4, waiting for transfers between devices: 0.01 us -> 1.08 us  [the longest x1 1.07 us: body(): other = lax.ppermute(got, 'user', [(i, i ^ 1) for i in range(peers)])]
    all_to_all x1, starting transfers between devices: 7.08 us -> 7.4 us  [body(): lax.all_to_all(packed, ('tm', 'user'), split_axis=0, concat_axis=0, tiled...]
  transfers between devices with their start and end apart: 4 -> 5, of which waited for: 1 -> 2; matrix products, arithmetic and copies ran while one was open for 0% -> 0% of each run, Pallas kernels for 17% -> 19%
where the time goes in v4:
time: 29.2 us; the launch traced here: 28.7 us
  starting transfers between devices  12.2 us (42%)
  Pallas kernels  9.39 us (32%)
  waiting for transfers between devices  5.73 us (20%)
  between operations  1.34 us (5%)
    all_to_all x1, starting transfers between devices, body(): lax.all_to_all(packed, ('tm', 'user'), split_axis=0, concat_axis=0, tiled...  7.4 us
    all_to_all x1, waiting for transfers between devices, body(): lax.all_to_all(packed, ('tm', 'user'), split_axis=0, concat_axis=0, tiled...  4.65 us
    pallas_call x1, Pallas kernels, body(): pl.pallas_call(functools.partial(user_kernel, dims), out_shape=shape(user...  3.14 us
    ppermute x1, starting transfers between devices, body(): other = lax.ppermute(got, 'user', [(i, i ^ 1) for i in range(peers)])  2.63 us
    pallas_call x1, Pallas kernels, body(): pl.pallas_call(gram_kernel, out_shape=near((groups, 2 * SUB * blocks, 2 *...  2.31 us
    ppermute x3, starting transfers between devices, body(): lax.ppermute(partial, 'user', [(i, i ^ d) for i in range(peers)])  2.21 us
    pallas_call x1, Pallas kernels, body(): pl.pallas_call(functools.partial(partial_kernel, dims), out_shape=(near((...  1.73 us
    pallas_call x1, Pallas kernels, body(): pl.pallas_call(functools.partial(pack_kernel, dims), out_shape=shape((tm...  1.57 us
  transfers between devices with their start and end apart: 5, of which 2 were waited for; matrix products, arithmetic and copies ran while one was open for 0% of the time, Pallas kernels for 19%

profile of v4, /device:TPU:1, one launch (start us, length us, event | category | flops | bytes accessed | tf_op | source)
XLA Modules:
  0.0 28.7 jit_solution(7726022733329249751)
XLA Ops:
  1.3 1.6 %pack.1 = bf16[16,48,128]{2,1,0:T(8,128)(2,1)} custom-call(bf16[64,128]{1,0:T(8,128)(2,1)} %v_ref.3, bf16[64,128]{1,0:T(8,128)(2,1)} %dv_ref.3, bf16[16,128]{1,0:T(8,128)(2,1)} %w_ref.3, bf16[16,128]{1,0:T(8,128)(2,1)} %dw_ref.3, s32[1,1,4,4]{3,2,1,0:T(4,128)} %send_ref.1, s32[1,1,16]{2,1,0:T(1,128)} %slot_ref.1, s32[1,1,16]{2,1,0:T(1,128)} %item_ref.1, ...), custom_call_target="tpu_custom_call" | custom-call | tf_op jit(solution)/shard_map/pack/pallas_call | solution.py:314
  2.8 7.4 %all-to-all-start = ((bf16[16,48,128]{2,1,0:T(8,128)(2,1)}), bf16[16,48,128]{2,1,0:T(8,128)(2,1)S(1)}, u32[]{:S(2)}, u32[]{:S(2)}) async-start(bf16[16,48,128]{2,1,0:T(8,128)(2,1)} %pack.1), calls=%async_computation | async-start | bytes 393216 | tf_op jit(solution)/shard_map/all_to_all | solution.py:331
  10.3 2.3 %grams.1.gram_ref = bf16[16,256,256]{2,1,0:T(8,128)(2,1)S(1)} custom-call(bf16[2048,128]{1,0:T(8,128)(2,1)} %u_hbm.1, bf16[2048,128]{1,0:T(8,128)(2,1)} %du_hbm.1), custom_call_target="tpu_custom_call" | custom-call | tf_op jit(solution)/shard_map/grams/pallas_call | solution.py:323
  12.6 4.7 %all-to-all-done.got_ref = bf16[16,48,128]{2,1,0:T(8,128)(2,1)S(1)} async-done(((bf16[16,48,128]{2,1,0:T(8,128)(2,1)}), bf16[16,48,128]{2,1,0:T(8,128)(2,1)S(1)}, u32[]{:S(2)}, u32[]{:S(2)}) %all-to-all-start) | async-done | bytes 196640 | tf_op jit(solution)/shard_map/all_to_all | solution.py:331
  17.2 2.6 %collective-permute-start = (bf16[16,48,128]{2,1,0:T(8,128)(2,1)S(1)}, bf16[16,48,128]{2,1,0:T(8,128)(2,1)S(1)}, u32[]{:S(2)}, u32[]{:S(2)}) collective-permute-start(bf16[16,48,128]{2,1,0:T(8,128)(2,1)S(1)} %all-to-all-done.got_ref), channel_id=1, source_target_pairs={{0,1},{1,0},{2,3},{3,2},{4,5},{5,4},{6,7},{7,6},{8,9},{9,8},{10,11... | collective-permute-start | bytes 589832 | tf_op jit(solution)/shard_map/ppermute | solution.py:335
  19.9 1.1 %collective-permute-done.other_ref = bf16[16,48,128]{2,1,0:T(8,128)(2,1)S(1)} collective-permute-done((bf16[16,48,128]{2,1,0:T(8,128)(2,1)S(1)}, bf16[16,48,128]{2,1,0:T(8,128)(2,1)S(1)}, u32[]{:S(2)}, u32[]{:S(2)}) %collective-permute-start) | collective-permute-done | bytes 196640 | tf_op jit(solution)/shard_map/ppermute | solution.py:335
  20.9 1.7 %partials.1 = (f32[80,128]{1,0:T(8,128)S(1)}, bf16[1,256,128]{2,1,0:T(8,128)(2,1)S(1)}, bf16[1,128,128]{2,1,0:T(8,128)(2,1)S(1)}, f32[2,256,128]{2,1,0:T(8,128)S(1)}, s32[1,8,128]{2,1,0:T(8,128)S(1)}) custom-call(bf16[16,48,128]{2,1,0:T(8,128)(2,1)S(1)} %all-to-all-done.got_ref, bf16[16,48,128]{2,1,0:T(8,128)(2,1)S(1)} %collective-permute-done.other_ref, ...), custom_call_target="tpu_custom_call" | custom-call | tf_op jit(solution)/shard_map/partials/pallas_call | solution.py:336
  22.7 1.0 %collective-permute-start.3 = (f32[80,128]{1,0:T(8,128)S(1)}, f32[80,128]{1,0:T(8,128)S(1)}, u32[]{:S(2)}, u32[]{:S(2)}) collective-permute-start(f32[80,128]{1,0:T(8,128)S(1)} %get-tuple-element.18.refs_0_), channel_id=1, source_target_pairs={{0,3},{1,2},{2,1},{3,0},{4,7},{5,6},{6,5},{7,4},{8,11},{9,10},{10,... | collective-permute-start | bytes 122888 | tf_op jit(solution)/shard_map/ppermute | solution.py:353
  23.7 0.8 %collective-permute-start.2 = (f32[80,128]{1,0:T(8,128)S(1)}, f32[80,128]{1,0:T(8,128)S(1)}, u32[]{:S(2)}, u32[]{:S(2)}) collective-permute-start(f32[80,128]{1,0:T(8,128)S(1)} %get-tuple-element.18.refs_0_), channel_id=1, source_target_pairs={{0,2},{1,3},{2,0},{3,1},{4,6},{5,7},{6,4},{7,5},{8,10},{9,11},{10,... | collective-permute-start | bytes 122888 | tf_op jit(solution)/shard_map/ppermute | solution.py:353
  24.5 0.4 %collective-permute-start.1 = (f32[80,128]{1,0:T(8,128)S(1)}, f32[80,128]{1,0:T(8,128)S(1)}, u32[]{:S(2)}, u32[]{:S(2)}) collective-permute-start(f32[80,128]{1,0:T(8,128)S(1)} %get-tuple-element.18.refs_0_), channel_id=1, source_target_pairs={{0,1},{1,0},{2,3},{3,2},{4,5},{5,4},{6,7},{7,6},{8,9},{9,8},{10,11... | collective-permute-start | bytes 122888 | tf_op jit(solution)/shard_map/ppermute | solution.py:353
  24.9 3.1 %user_rows.1 = f32[2048,128]{1,0:T(8,128)} custom-call(bf16[2048,128]{1,0:T(8,128)(2,1)} %u_hbm.1, bf16[2048,128]{1,0:T(8,128)(2,1)} %du_hbm.1, bf16[1,256,128]{2,1,0:T(8,128)(2,1)S(1)} %get-tuple-element.14.wt_ref, bf16[1,128,128]{2,1,0:T(8,128)(2,1)S(1)} %get-tuple-element.15.ww_ref, f32[2,256,128]{2,1,0:T(8,128)S(1)} %get-tuple-element.16.gh_ref, ...), custom_call_target="tpu_custom_call" | custom-call | tf_op jit(solution)/shard_map/user_rows/pallas_call | solution.py:354
  28.0 0.0 collective-permute-done.3.refs_3_
  28.0 0.0 collective-permute-done.2.refs_2_
  28.0 0.0 collective-permute-done.1.refs_1_
  28.1 0.6 %finish.1 = (f32[64,128]{1,0:T(8,128)}, f32[16,128]{1,0:T(8,128)}) custom-call(f32[80,128]{1,0:T(8,128)S(1)} %get-tuple-element.18.refs_0_, f32[80,128]{1,0:T(8,128)S(1)} %collective-permute-done.1.refs_1_, f32[80,128]{1,0:T(8,128)S(1)} %collective-permute-done.2.refs_2_, f32[80,128]{1,0:T(8,128)S(1)} %collective-permute-done.3.refs_3_), custom_call_target="tpu_custom_call" | custom-call | tf_op jit(solution)/shard_map/finish/pallas_call | solution.py:370
Async XLA Ops:
  2.8 14.4 %all-to-all-start = ((bf16[16,48,128]{2,1,0:T(8,128)(2,1)}), bf16[16,48,128]{2,1,0:T(8,128)(2,1)S(1)}, u32[]{:S(2)}, u32[]{:S(2)}) async-start(bf16[16,48,128]{2,1,0:T(8,128)(2,1)} %pack.1), calls=%async_computation | async-start | bytes 393216 | tf_op jit(solution)/shard_map/all_to_all | solution.py:331
  17.2 3.7 %collective-permute-start = (bf16[16,48,128]{2,1,0:T(8,128)(2,1)S(1)}, bf16[16,48,128]{2,1,0:T(8,128)(2,1)S(1)}, u32[]{:S(2)}, u32[]{:S(2)}) collective-permute-start(bf16[16,48,128]{2,1,0:T(8,128)(2,1)S(1)} %all-to-all-done.got_ref), channel_id=1, source_target_pairs={{0,1},{1,0},{2,3},{3,2},{4,5},{5,4},{6,7},{7,6},{8,9},{9,8},{10,11... | collective-permute-start | bytes 589832 | tf_op jit(solution)/shard_map/ppermute | solution.py:335
  22.7 5.4 %collective-permute-start.3 = (f32[80,128]{1,0:T(8,128)S(1)}, f32[80,128]{1,0:T(8,128)S(1)}, u32[]{:S(2)}, u32[]{:S(2)}) collective-permute-start(f32[80,128]{1,0:T(8,128)S(1)} %get-tuple-element.18.refs_0_), channel_id=1, source_target_pairs={{0,3},{1,2},{2,1},{3,0},{4,7},{5,6},{6,5},{7,4},{8,11},{9,10},{10,... | collective-permute-start | bytes 122888 | tf_op jit(solution)/shard_map/ppermute | solution.py:353
  23.7 4.4 %collective-permute-start.2 = (f32[80,128]{1,0:T(8,128)S(1)}, f32[80,128]{1,0:T(8,128)S(1)}, u32[]{:S(2)}, u32[]{:S(2)}) collective-permute-start(f32[80,128]{1,0:T(8,128)S(1)} %get-tuple-element.18.refs_0_), channel_id=1, source_target_pairs={{0,2},{1,3},{2,0},{3,1},{4,6},{5,7},{6,4},{7,5},{8,10},{9,11},{10,... | collective-permute-start | bytes 122888 | tf_op jit(solution)/shard_map/ppermute | solution.py:353
  24.5 3.6 %collective-permute-start.1 = (f32[80,128]{1,0:T(8,128)S(1)}, f32[80,128]{1,0:T(8,128)S(1)}, u32[]{:S(2)}, u32[]{:S(2)}) collective-permute-start(f32[80,128]{1,0:T(8,128)S(1)} %get-tuple-element.18.refs_0_), channel_id=1, source_target_pairs={{0,1},{1,0},{2,3},{3,2},{4,5},{5,4},{6,7},{7,6},{8,9},{9,8},{10,11... | collective-permute-start | bytes 122888 | tf_op jit(solution)/shard_map/ppermute | solution.py:353

commit v5 on v4

--- a/solution.py
+++ b/solution.py
@@ -115,7 +115,7 @@
         out_ref[at + a + 1] = both[:, R:]
 
 
-def partial_kernel(dims, got_ref, other_ref, gram_ref, v_ref, dv_ref, w_ref, dw_ref, out_ref, wt_ref, ww_ref, gh_ref, entry_ref, left_ref, grams_ref):
+def partial_kernel(dims, got_ref, other_ref, gram_ref, out_ref, wt_ref, ww_ref, gh_ref, entry_ref, left_ref, grams_ref):
     tm, peers, tiles, steps, rows = dims
     groups, depth = gram_ref.shape[:2]
     blocks = depth // (2 * SUB)
@@ -190,7 +190,7 @@
             )
 
         v = gathered(0)
-        gh_ref[m] = dot_tn(jnp.concatenate([v, gathered(part)], axis=1), v)
+        gh_ref[m] = OBS_WEIGHT * dot_tn(jnp.concatenate([v, gathered(part)], axis=1), v)
         return carry
 
     lax.fori_loop(0, tiles, item_grams, 0, unroll=tiles <= 2)
@@ -214,12 +214,15 @@
             r_rows = r_rows + s[here] * g_m
         for side, value in zip(sides, (a_rows, b_rows, q_rows, r_rows)):
             side.append(value)
-    left = jnp.concatenate([v_ref[...], dv_ref[...]], axis=1)
+    v_own = jnp.concatenate([sent(me_tm, j, 0, part) for j in range(peers)], axis=0)
+    dv_own = jnp.concatenate([sent(me_tm, j, part, 2 * part) for j in range(peers)], axis=0)
+    left = jnp.concatenate([v_own, dv_own], axis=1)
     item_rows = OBS_WEIGHT * dot_split(left, jnp.concatenate(sides[0] + sides[1], axis=0))
-    left = jnp.concatenate([w_ref[...], dw_ref[...]], axis=1)
-    time_rows = OBS_WEIGHT * dot_split(left, jnp.concatenate(sides[2] + sides[3], axis=0))
+    own = [sent(me_tm, j, 2 * part, 2 * part + 16).astype(F32)[:piece] for j in range(peers)]
+    left = jnp.concatenate([jnp.concatenate(own[:half], axis=0), jnp.concatenate(own[half:], axis=0)], axis=1)
+    time_rows = dot_split(left.astype(BF16), jnp.concatenate(sides[2] + sides[3], axis=0))
     first = jnp.where(me == 0, 1.0, 0.0)
-    out_ref[:rows, :] = item_rows + (first * LAMBDA_ITEM) * dv_ref[...].astype(F32)
+    out_ref[:rows, :] = item_rows + (first * LAMBDA_ITEM) * dv_own.astype(F32)
     out_ref[rows:, :] = time_rows + (first * LAMBDA_TIME) * penalty
 
 
@@ -244,9 +247,9 @@
         place = iota(shape_right, 0) // SUB
         right = (iota(shape_right, 1) // steps == place // width) & (item == first + place % width)
         counts = count_rows(left, right, True)
-        for group in range(groups):
-            at = pl.ds(group * SUB, SUB)
-            below = pl.ds(R + group * SUB, SUB)
+        def rows_of(group, carry):
+            at = pl.ds(pl.multiple_of(group * SUB, SUB), SUB)
+            below = pl.ds(pl.multiple_of(R + group * SUB, SUB), SUB)
             stack = []
             for a in range(entries):
                 y, z = grams_ref[a, at, :], grams_ref[a, below, :]
@@ -255,7 +258,13 @@
                     stack.append(jnp.concatenate([g_m * y, g_m * z + h_m * y], axis=1))
             high, low = halves(jnp.concatenate(stack, axis=0))
             value = dot_nn(counts, jnp.concatenate([high, low], axis=0)).reshape(blocks, SUB, 2 * R)
+            if fresh:
+                eye = iota((SUB, 2 * R), 0) + group * SUB == iota((SUB, 2 * R), 1)
+                value = value + jnp.where(eye, LAMBDA_USER, 0.0)[None]
             k_ref[:, at, :] = value if fresh else k_ref[:, at, :] + value
+            return carry
+
+        lax.fori_loop(0, groups, rows_of, 0, unroll=8)
 
     for chunk in range(chunks):
         time_grams(wt_ref[chunk], ww_ref[chunk], grams_ref, 0, steps)
@@ -274,10 +283,8 @@
     for number in range(out_sem.shape[0]):
         for g in range(number * per_store, (number + 1) * per_store):
             at = pl.ds(g * UB, UB)
-            du = du_ref[at, :]
-            left = jnp.concatenate([du, u_ref[at, :]], axis=1)
-            term = dot_split(left, jnp.concatenate([k_ref[g, :, :R], k_ref[g, :, R:]], axis=0))
-            out_ref[at, :] = OBS_WEIGHT * term + LAMBDA_USER * du.astype(F32)
+            left = jnp.concatenate([du_ref[at, :], u_ref[at, :]], axis=1)
+            out_ref[at, :] = dot_split(left, jnp.concatenate([k_ref[g, :, :R], k_ref[g, :, R:]], axis=0))
         at = pl.ds(number * per_store * UB, per_store * UB)
         store = pltpu.make_async_copy(out_ref.at[at, :], out_hbm.at[at, :], out_sem.at[number])
         store.start()
@@ -342,14 +349,14 @@
             near((tiles, 2 * R, R), F32),
             near((chunks, 8, LANES), jnp.int32),
         ),
-        in_specs=[VM] * 7,
+        in_specs=[VM] * 3,
         out_specs=(VM,) * 5,
         scratch_shapes=[
             pltpu.VMEM(((tm + tiles) * SUB, 2 * SUB * blocks), BF16),
             pltpu.VMEM((tm, 2 * R, R), F32),
         ],
         name="partials",
-    )(*held(got, other, grams), item_factor, item_tangent, time_factor, time_tangent)
+    )(*held(got, other, grams))
     others = [lax.ppermute(partial, "user", [(i, i ^ d) for i in range(peers)]) for d in range(1, peers)]
     user_hvp = pl.pallas_call(
         functools.partial(user_kernel, dims),

time: 29.2 us -> 28.1 us (0.962)
  the two profiles are of different devices: /device:TPU:1 before, /device:TPU:0 now
where the time goes in v5:
time: 28.1 us; the launch traced here: 27.7 us
  starting transfers between devices  10.3 us (37%)
  waiting for transfers between devices  8.13 us (29%)
  Pallas kernels  8.02 us (29%)
  between operations  1.32 us (5%)
    all_to_all x1, starting transfers between devices, body(): lax.all_to_all(packed, ('tm', 'user'), split_axis=0, concat_axis=0, tiled...  8.34 us
    all_to_all x1, waiting for transfers between devices, body(): lax.all_to_all(packed, ('tm', 'user'), split_axis=0, concat_axis=0, tiled...  6.33 us
    pallas_call x1, Pallas kernels, body(): pl.pallas_call(functools.partial(user_kernel, dims), out_shape=shape(user...  2.51 us
    pallas_call x1, Pallas kernels, body(): pl.pallas_call(gram_kernel, out_shape=near((groups, 2 * SUB * blocks, 2 *...  2.3 us
    ppermute x3, starting transfers between devices, body(): lax.ppermute(partial, 'user', [(i, i ^ d) for i in range(peers)])  1.93 us
    pallas_call x1, Pallas kernels, body(): pl.pallas_call(functools.partial(pack_kernel, dims), out_shape=shape((tm...  1.57 us
    ppermute x1, waiting for transfers between devices, body(): other = lax.ppermute(got, 'user', [(i, i ^ 1) for i in range(peers)])  1.44 us
    pallas_call x1, Pallas kernels, body(): pl.pallas_call(functools.partial(partial_kernel, dims), out_shape=(near((...  1.01 us
  transfers between devices with their start and end apart: 5, of which 3 were waited for; matrix products, arithmetic and copies ran while one was open for 0% of the time, Pallas kernels for 17%

profile of v5, /device:TPU:0, one launch (start us, length us, event | category | flops | bytes accessed | tf_op | source)
XLA Modules:
  0.0 27.7 jit_solution(3666768729403647474)
XLA Ops:
  1.3 1.6 %pack.1 = bf16[16,48,128]{2,1,0:T(8,128)(2,1)} custom-call(bf16[64,128]{1,0:T(8,128)(2,1)} %v_ref.1, bf16[64,128]{1,0:T(8,128)(2,1)} %dv_ref.1, bf16[16,128]{1,0:T(8,128)(2,1)} %w_ref.1, bf16[16,128]{1,0:T(8,128)(2,1)} %dw_ref.1, s32[1,1,4,4]{3,2,1,0:T(4,128)} %send_ref.1, s32[1,1,16]{2,1,0:T(1,128)} %slot_ref.1, s32[1,1,16]{2,1,0:T(1,128)} %item_ref.1, ...), custom_call_target="tpu_custom_call" | custom-call | tf_op jit(solution)/shard_map/pack/pallas_call | solution.py:321
  2.9 8.3 %all-to-all-start = ((bf16[16,48,128]{2,1,0:T(8,128)(2,1)}), bf16[16,48,128]{2,1,0:T(8,128)(2,1)S(1)}, u32[]{:S(2)}, u32[]{:S(2)}) async-start(bf16[16,48,128]{2,1,0:T(8,128)(2,1)} %pack.1), calls=%async_computation | async-start | bytes 393216 | tf_op jit(solution)/shard_map/all_to_all | solution.py:338
  11.2 2.3 %grams.1.gram_ref = bf16[16,256,256]{2,1,0:T(8,128)(2,1)S(1)} custom-call(bf16[2048,128]{1,0:T(8,128)(2,1)} %u_hbm.1, bf16[2048,128]{1,0:T(8,128)(2,1)} %du_hbm.1), custom_call_target="tpu_custom_call" | custom-call | tf_op jit(solution)/shard_map/grams/pallas_call | solution.py:330
  13.5 6.3 %all-to-all-done.got_ref = bf16[16,48,128]{2,1,0:T(8,128)(2,1)S(1)} async-done(((bf16[16,48,128]{2,1,0:T(8,128)(2,1)}), bf16[16,48,128]{2,1,0:T(8,128)(2,1)S(1)}, u32[]{:S(2)}, u32[]{:S(2)}) %all-to-all-start) | async-done | bytes 196640 | tf_op jit(solution)/shard_map/all_to_all | solution.py:338
  19.8 0.0 collective-permute-start
  19.8 1.4 %collective-permute-done.other_ref = bf16[16,48,128]{2,1,0:T(8,128)(2,1)S(1)} collective-permute-done((bf16[16,48,128]{2,1,0:T(8,128)(2,1)S(1)}, bf16[16,48,128]{2,1,0:T(8,128)(2,1)S(1)}, u32[]{:S(2)}, u32[]{:S(2)}) %collective-permute-start) | collective-permute-done | bytes 196640 | tf_op jit(solution)/shard_map/ppermute | solution.py:342
  21.3 1.0 %partials.1 = (f32[80,128]{1,0:T(8,128)S(1)}, bf16[1,256,128]{2,1,0:T(8,128)(2,1)S(1)}, bf16[1,128,128]{2,1,0:T(8,128)(2,1)S(1)}, f32[2,256,128]{2,1,0:T(8,128)S(1)}, s32[1,8,128]{2,1,0:T(8,128)S(1)}) custom-call(bf16[16,48,128]{2,1,0:T(8,128)(2,1)S(1)} %all-to-all-done.got_ref, bf16[16,48,128]{2,1,0:T(8,128)(2,1)S(1)} %collective-permute-done.other_ref, ...), custom_call_target="tpu_custom_call" | custom-call | tf_op jit(solution)/shard_map/partials/pallas_call | solution.py:343
  22.3 0.7 %collective-permute-start.3 = (f32[80,128]{1,0:T(8,128)S(1)}, f32[80,128]{1,0:T(8,128)S(1)}, u32[]{:S(2)}, u32[]{:S(2)}) collective-permute-start(f32[80,128]{1,0:T(8,128)S(1)} %get-tuple-element.18.refs_0_), channel_id=1, source_target_pairs={{0,3},{1,2},{2,1},{3,0},{4,7},{5,6},{6,5},{7,4},{8,11},{9,10},{10,... | collective-permute-start | bytes 122888 | tf_op jit(solution)/shard_map/ppermute | solution.py:360
  23.0 1.1 %collective-permute-start.2 = (f32[80,128]{1,0:T(8,128)S(1)}, f32[80,128]{1,0:T(8,128)S(1)}, u32[]{:S(2)}, u32[]{:S(2)}) collective-permute-start(f32[80,128]{1,0:T(8,128)S(1)} %get-tuple-element.18.refs_0_), channel_id=1, source_target_pairs={{0,2},{1,3},{2,0},{3,1},{4,6},{5,7},{6,4},{7,5},{8,10},{9,11},{10,... | collective-permute-start | bytes 122888 | tf_op jit(solution)/shard_map/ppermute | solution.py:360
  24.1 0.1 collective-permute-start.1
  24.2 2.5 %user_rows.1 = f32[2048,128]{1,0:T(8,128)} custom-call(bf16[2048,128]{1,0:T(8,128)(2,1)} %u_hbm.1, bf16[2048,128]{1,0:T(8,128)(2,1)} %du_hbm.1, bf16[1,256,128]{2,1,0:T(8,128)(2,1)S(1)} %get-tuple-element.14.wt_ref, bf16[1,128,128]{2,1,0:T(8,128)(2,1)S(1)} %get-tuple-element.15.ww_ref, f32[2,256,128]{2,1,0:T(8,128)S(1)} %get-tuple-element.16.gh_ref, ...), custom_call_target="tpu_custom_call" | custom-call | tf_op jit(solution)/shard_map/user_rows/pallas_call | solution.py:361
  26.7 0.0 collective-permute-done.3.refs_3_
  26.8 0.4 %collective-permute-done.2.refs_2_ = f32[80,128]{1,0:T(8,128)S(1)} collective-permute-done((f32[80,128]{1,0:T(8,128)S(1)}, f32[80,128]{1,0:T(8,128)S(1)}, u32[]{:S(2)}, u32[]{:S(2)}) %collective-permute-start.2) | collective-permute-done | bytes 40992 | tf_op jit(solution)/shard_map/ppermute | solution.py:360
  27.1 0.0 collective-permute-done.1.refs_1_
  27.1 0.6 %finish.1 = (f32[64,128]{1,0:T(8,128)}, f32[16,128]{1,0:T(8,128)}) custom-call(f32[80,128]{1,0:T(8,128)S(1)} %get-tuple-element.18.refs_0_, f32[80,128]{1,0:T(8,128)S(1)} %collective-permute-done.1.refs_1_, f32[80,128]{1,0:T(8,128)S(1)} %collective-permute-done.2.refs_2_, f32[80,128]{1,0:T(8,128)S(1)} %collective-permute-done.3.refs_3_), custom_call_target="tpu_custom_call" | custom-call | tf_op jit(solution)/shard_map/finish/pallas_call | solution.py:377
Async XLA Ops:
  2.9 17.0 %all-to-all-start = ((bf16[16,48,128]{2,1,0:T(8,128)(2,1)}), bf16[16,48,128]{2,1,0:T(8,128)(2,1)S(1)}, u32[]{:S(2)}, u32[]{:S(2)}) async-start(bf16[16,48,128]{2,1,0:T(8,128)(2,1)} %pack.1), calls=%async_computation | async-start | bytes 393216 | tf_op jit(solution)/shard_map/all_to_all | solution.py:338
  19.8 1.4 %collective-permute-start = (bf16[16,48,128]{2,1,0:T(8,128)(2,1)S(1)}, bf16[16,48,128]{2,1,0:T(8,128)(2,1)S(1)}, u32[]{:S(2)}, u32[]{:S(2)}) collective-permute-start(bf16[16,48,128]{2,1,0:T(8,128)(2,1)S(1)} %all-to-all-done.got_ref), channel_id=1, source_target_pairs={{0,1},{1,0},{2,3},{3,2},{4,5},{5,4},{6,7},{7,6},{8,9},{9,8},{10,11... | collective-permute-start | bytes 589832 | tf_op jit(solution)/shard_map/ppermute | solution.py:342
  22.3 4.4 %collective-permute-start.3 = (f32[80,128]{1,0:T(8,128)S(1)}, f32[80,128]{1,0:T(8,128)S(1)}, u32[]{:S(2)}, u32[]{:S(2)}) collective-permute-start(f32[80,128]{1,0:T(8,128)S(1)} %get-tuple-element.18.refs_0_), channel_id=1, source_target_pairs={{0,3},{1,2},{2,1},{3,0},{4,7},{5,6},{6,5},{7,4},{8,11},{9,10},{10,... | collective-permute-start | bytes 122888 | tf_op jit(solution)/shard_map/ppermute | solution.py:360
  23.0 4.1 %collective-permute-start.2 = (f32[80,128]{1,0:T(8,128)S(1)}, f32[80,128]{1,0:T(8,128)S(1)}, u32[]{:S(2)}, u32[]{:S(2)}) collective-permute-start(f32[80,128]{1,0:T(8,128)S(1)} %get-tuple-element.18.refs_0_), channel_id=1, source_target_pairs={{0,2},{1,3},{2,0},{3,1},{4,6},{5,7},{6,4},{7,5},{8,10},{9,11},{10,... | collective-permute-start | bytes 122888 | tf_op jit(solution)/shard_map/ppermute | solution.py:360
  24.1 3.0 %collective-permute-start.1 = (f32[80,128]{1,0:T(8,128)S(1)}, f32[80,128]{1,0:T(8,128)S(1)}, u32[]{:S(2)}, u32[]{:S(2)}) collective-permute-start(f32[80,128]{1,0:T(8,128)S(1)} %get-tuple-element.18.refs_0_), channel_id=1, source_target_pairs={{0,1},{1,0},{2,3},{3,2},{4,5},{5,4},{6,7},{7,6},{8,9},{9,8},{10,11... | collective-permute-start | bytes 122888 | tf_op jit(solution)/shard_map/ppermute | solution.py:360

commit v6 on v5

--- a/solution.py
+++ b/solution.py
@@ -53,25 +53,27 @@
     me = lax.axis_index("user")
     part = rows // peers
     start = pl.multiple_of(me * part, part)
-    time_ref[0:steps, :] = w_ref[...].astype(F32)
-    time_ref[steps:, :] = dw_ref[...].astype(F32)
-    piece = 2 * steps // peers
-    time_rows = time_ref[pl.ds(pl.multiple_of(me * piece, piece), piece), :]
+    time_ref[0, :, :] = w_ref[...].astype(F32)
+    time_ref[1, :, :] = dw_ref[...].astype(F32)
     slots = send_ref.shape[3]
-    row, lane = iota((8, LANES), 0), iota((8, LANES), 1)
-    wanted = row * slots + lane % slots
-    table = jnp.full((8, LANES), -1, jnp.int32)
-    count = count_ref[0, 0]
-    for n in range(slot_ref.shape[2]):
-        hit = (wanted == slot_ref[0, 0, n]) & (n < count)
-        table = jnp.where(hit, item_ref[0, 0, n], table)
+    row, lane = iota((SUB, LANES), 0), iota((SUB, LANES), 1)
+    sent_list = jnp.zeros((SUB, LANES), jnp.int32)
     entry = lane % (peers * slots)
     for j in range(peers):
         for s in range(slots):
-            table = jnp.where((row == peers) & (entry == j * slots + s), send_ref[0, 0, j, s], table)
-    last = jnp.concatenate([time_rows, table.astype(F32)], axis=0).astype(BF16)
-    whole = jnp.concatenate([v_ref[pl.ds(start, part), :], dv_ref[pl.ds(start, part), :], last], axis=0)
-    out_ref[...] = jnp.broadcast_to(whole[None], out_ref.shape)
+            sent_list = jnp.where(entry == j * slots + s, send_ref[0, 0, j, s], sent_list)
+    count = count_ref[0, 0]
+    at = pl.multiple_of(me // 2 * SUB, SUB)
+    for k in range(peers):
+        table = jnp.full((SUB, LANES), -1, jnp.int32)
+        for n in range(slot_ref.shape[2]):
+            hit = (lane % slots + k * slots == slot_ref[0, 0, n]) & (n < count)
+            table = jnp.where(hit, item_ref[0, 0, n], table)
+        lists = jnp.where(row % 4 == 0, table, sent_list).astype(F32)
+        last = jnp.where(row // 4 == me % 2, time_ref[k % 2, pl.ds(at, SUB), :], lists).astype(BF16)
+        first = (dv_ref if k % 2 else v_ref)[pl.ds(start, part), :]
+        out_ref[:, k, :part, :] = jnp.broadcast_to(first[None], (tm, part, R))
+        out_ref[:, k, part:, :] = jnp.broadcast_to(last[None], (tm, SUB, R))
 
 
 def gram_kernel(u_ref, du_ref, out_ref):
@@ -120,16 +122,24 @@
     groups, depth = gram_ref.shape[:2]
     blocks = depth // (2 * SUB)
     part = rows // peers
-    piece = 2 * steps // peers
     entries = LANES // steps
     chunks = tm // entries
     me_tm, me = lax.axis_index("tm"), lax.axis_index("user")
     lane, row8 = iota((8, LANES), 1), iota((8, LANES), 0)
     slots = steps // peers
-
-    def sent(a, j, first, last):
-        here = a * (peers // 2) + j // 2
-        return jnp.where(me % 2 == j % 2, got_ref[here, first:last, :], other_ref[here, first:last, :])
+    even = me % 2 == 0
+
+    def sent(a, j, kind):
+        here = a * peers + j
+        return jnp.where(even == (kind == 0), got_ref[here, :part, :], other_ref[here, :part, :])
+
+    def time_rows_of(a):
+        lasts = [[ref[a * peers + j, part:, :].astype(F32) for j in range(peers)] for ref in (got_ref, other_ref)]
+        sides = []
+        for kind in range(2):
+            pieces = [jnp.where(even == (kind == 0), lasts[0][j], lasts[1][j]) for j in range(peers)]
+            sides.append(jnp.concatenate([jnp.where(row8 < 4, *pieces[j : j + 2]) for j in range(0, peers, 2)], axis=0))
+        return sides, lasts[0]
 
     my_tile = me_tm * rows // IT
 
@@ -140,21 +150,21 @@
     own_counts = jnp.zeros((tiles * SUB, blocks * SUB), BF16)
     for chunk in range(chunks):
         base = chunk * entries
-        pieces = []
         found_m = jnp.zeros((8, LANES), F32)
         found_g = jnp.zeros((8, LANES), F32)
+        sides = ([], [])
         for a in range(entries):
+            both, lasts = time_rows_of(base + a)
+            sides[0].append(both[0])
+            sides[1].append(both[1])
+            mine = lane // steps == a
             for j in range(peers):
-                tile = sent(base + a, j, 2 * part, 2 * part + 16).astype(F32)
-                pieces.append(tile[:piece])
-                mine = lane // steps == a
-                hit = mine & (row8 == me) & (lane // slots % peers == j)
-                found_m = found_m + jnp.where(hit, tile[piece:], 0.0)
-                hit = mine & (row8 == peers) & (me == j)
-                found_g = found_g + jnp.where(hit, tile[piece:], 0.0)
-        half = peers // 2
-        w = jnp.concatenate([pieces[a * peers + j] for a in range(entries) for j in range(half)], axis=0)
-        dw = jnp.concatenate([pieces[a * peers + j] for a in range(entries) for j in range(half, peers)], axis=0)
+                at = 0 if j % 2 else 4
+                hit = mine & (row8 == at) & (lane // slots % peers == j)
+                found_m = found_m + jnp.where(hit, lasts[j], 0.0)
+                hit = mine & (row8 == at + 1) & (me == j)
+                found_g = found_g + jnp.where(hit, lasts[j], 0.0)
+        w, dw = jnp.concatenate(sides[0], axis=0), jnp.concatenate(sides[1], axis=0)
         wt_ref[chunk] = jnp.concatenate([w, dw], axis=1).T.astype(BF16)
         ww_ref[chunk] = w.astype(BF16)
         time_grams(wt_ref[chunk], ww_ref[chunk], grams_ref, base, steps)
@@ -183,14 +193,11 @@
     per_tile = IT // rows
 
     def item_grams(m, carry):
-        def gathered(first):
-            return jnp.concatenate(
-                [sent(m * per_tile + a, j, first, first + part) for a in range(per_tile) for j in range(peers)],
-                axis=0,
-            )
+        def gathered(kind):
+            return jnp.concatenate([sent(m * per_tile + a, j, kind) for a in range(per_tile) for j in range(peers)], axis=0)
 
         v = gathered(0)
-        gh_ref[m] = OBS_WEIGHT * dot_tn(jnp.concatenate([v, gathered(part)], axis=1), v)
+        gh_ref[m] = OBS_WEIGHT * dot_tn(jnp.concatenate([v, gathered(1)], axis=1), v)
         return carry
 
     lax.fori_loop(0, tiles, item_grams, 0, unroll=tiles <= 2)
@@ -214,12 +221,11 @@
             r_rows = r_rows + s[here] * g_m
         for side, value in zip(sides, (a_rows, b_rows, q_rows, r_rows)):
             side.append(value)
-    v_own = jnp.concatenate([sent(me_tm, j, 0, part) for j in range(peers)], axis=0)
-    dv_own = jnp.concatenate([sent(me_tm, j, part, 2 * part) for j in range(peers)], axis=0)
+    v_own = jnp.concatenate([sent(me_tm, j, 0) for j in range(peers)], axis=0)
+    dv_own = jnp.concatenate([sent(me_tm, j, 1) for j in range(peers)], axis=0)
     left = jnp.concatenate([v_own, dv_own], axis=1)
     item_rows = OBS_WEIGHT * dot_split(left, jnp.concatenate(sides[0] + sides[1], axis=0))
-    own = [sent(me_tm, j, 2 * part, 2 * part + 16).astype(F32)[:piece] for j in range(peers)]
-    left = jnp.concatenate([jnp.concatenate(own[:half], axis=0), jnp.concatenate(own[half:], axis=0)], axis=1)
+    left = jnp.concatenate(time_rows_of(me_tm)[0], axis=1)
     time_rows = dot_split(left.astype(BF16), jnp.concatenate(sides[2] + sides[3], axis=0))
     first = jnp.where(me == 0, 1.0, 0.0)
     out_ref[:rows, :] = item_rows + (first * LAMBDA_ITEM) * dv_own.astype(F32)
@@ -317,13 +323,13 @@
     dims = (tm, peers, tiles, steps, rows)
     chunks = tm * steps // LANES
     near, held = placed(chunks == 1 and tiles <= 2)
-    height = 2 * rows // peers + 2 * steps // peers + 8
+    height = rows // peers + SUB
     packed = pl.pallas_call(
         functools.partial(pack_kernel, dims),
-        out_shape=shape((tm * peers // 2, height, R), BF16),
+        out_shape=shape((tm, peers, height, R), BF16),
         in_specs=[VM] * 4 + [SM] * 4,
         out_specs=VM,
-        scratch_shapes=[pltpu.VMEM((2 * steps, R), F32)],
+        scratch_shapes=[pltpu.VMEM((2, steps, R), F32)],
         name="pack",
     )(item_factor, item_tangent, time_factor, time_tangent, send_list, tile_slot, tile_item, tile_count)
     groups = R // SUB
@@ -334,9 +340,8 @@
         out_specs=VM,
         name="grams",
     )(user_factor, user_tangent)
-    cores = [[i for i in range(tm * peers) if i % 2 == core] for core in range(2)]
     got = lax.all_to_all(
-        packed, ("tm", "user"), split_axis=0, concat_axis=0, tiled=True, axis_index_groups=cores
+        packed.reshape(tm * peers, height, R), ("tm", "user"), split_axis=0, concat_axis=0, tiled=True
     )
     got, grams = lax.optimization_barrier((got, grams))
     other = lax.ppermute(got, "user", [(i, i ^ 1) for i in range(peers)])

time: 28.1 us -> 27.5 us (0.979)
  the two profiles are of different devices: /device:TPU:0 before, /device:TPU:1 now
where the time goes in v6:
time: 27.5 us; the launch traced here: 27 us
  starting transfers between devices  9.29 us (34%)
  waiting for transfers between devices  8.33 us (30%)
  Pallas kernels  8.07 us (29%)
  between operations  1.34 us (5%)
    all_to_all x1, starting transfers between devices, body(): lax.all_to_all(packed.reshape(tm * peers, height, R), ('tm', 'user'), spl...  7.08 us
    all_to_all x1, waiting for transfers between devices, body(): lax.all_to_all(packed.reshape(tm * peers, height, R), ('tm', 'user'), spl...  6.89 us
    pallas_call x1, Pallas kernels, body(): pl.pallas_call(functools.partial(user_kernel, dims), out_shape=shape(user...  2.51 us
    pallas_call x1, Pallas kernels, body(): pl.pallas_call(gram_kernel, out_shape=near((groups, 2 * SUB * blocks, 2 *...  2.31 us
    ppermute x3, starting transfers between devices, body(): lax.ppermute(partial, 'user', [(i, i ^ d) for i in range(peers)])  2.21 us
    pallas_call x1, Pallas kernels, body(): pl.pallas_call(functools.partial(pack_kernel, dims), out_shape=shape((tm,...  1.6 us
    ppermute x1, waiting for transfers between devices, body(): other = lax.ppermute(got, 'user', [(i, i ^ 1) for i in range(peers)])  1.44 us
    pallas_call x1, Pallas kernels, body(): pl.pallas_call(functools.partial(partial_kernel, dims), out_shape=(near((...  1.03 us
  transfers between devices with their start and end apart: 5, of which 2 were waited for; matrix products, arithmetic and copies ran while one was open for 0% of the time, Pallas kernels for 18%

profile of v6, /device:TPU:1, one launch (start us, length us, event | category | flops | bytes accessed | tf_op | source)
XLA Modules:
  0.0 27.0 jit_solution(15454426097041535834)
XLA Ops:
  1.3 1.6 %pack.1 = bf16[8,4,24,128]{3,2,1,0:T(8,128)(2,1)} custom-call(bf16[64,128]{1,0:T(8,128)(2,1)} %v_ref.1, bf16[64,128]{1,0:T(8,128)(2,1)} %dv_ref.1, bf16[16,128]{1,0:T(8,128)(2,1)} %w_ref.1, bf16[16,128]{1,0:T(8,128)(2,1)} %dw_ref.1, s32[1,1,4,4]{3,2,1,0:T(4,128)} %send_ref.1, s32[1,1,16]{2,1,0:T(1,128)} %slot_ref.1, s32[1,1,16]{2,1,0:T(1,128)} %item_ref.1, ...), custom_call_target="tpu_custom_call" | custom-call | tf_op jit(solution)/shard_map/pack/pallas_call | solution.py:327
  2.9 7.1 %all-to-all-start = ((bf16[32,24,128]{2,1,0:T(8,128)(2,1)}), bf16[32,24,128]{2,1,0:T(8,128)(2,1)S(1)}, u32[]{:S(2)}, u32[]{:S(2)}) async-start(bf16[32,24,128]{2,1,0:T(8,128)(2,1)} %bitcast.1), calls=%async_computation | async-start | bytes 393216 | tf_op jit(solution)/shard_map/all_to_all | solution.py:343
  10.0 2.3 %grams.1.gram_ref = bf16[16,256,256]{2,1,0:T(8,128)(2,1)S(1)} custom-call(bf16[2048,128]{1,0:T(8,128)(2,1)} %u_hbm.1, bf16[2048,128]{1,0:T(8,128)(2,1)} %du_hbm.1), custom_call_target="tpu_custom_call" | custom-call | tf_op jit(solution)/shard_map/grams/pallas_call | solution.py:336
  12.3 6.9 %all-to-all-done.got_ref = bf16[32,24,128]{2,1,0:T(8,128)(2,1)S(1)} async-done(((bf16[32,24,128]{2,1,0:T(8,128)(2,1)}), bf16[32,24,128]{2,1,0:T(8,128)(2,1)S(1)}, u32[]{:S(2)}, u32[]{:S(2)}) %all-to-all-start) | async-done | bytes 196640 | tf_op jit(solution)/shard_map/all_to_all | solution.py:343
  19.2 0.0 collective-permute-start
  19.2 1.4 %collective-permute-done.other_ref = bf16[32,24,128]{2,1,0:T(8,128)(2,1)S(1)} collective-permute-done((bf16[32,24,128]{2,1,0:T(8,128)(2,1)S(1)}, bf16[32,24,128]{2,1,0:T(8,128)(2,1)S(1)}, u32[]{:S(2)}, u32[]{:S(2)}) %collective-permute-start) | collective-permute-done | bytes 196640 | tf_op jit(solution)/shard_map/ppermute | solution.py:347
  20.6 1.0 %partials.1 = (f32[80,128]{1,0:T(8,128)S(1)}, bf16[1,256,128]{2,1,0:T(8,128)(2,1)S(1)}, bf16[1,128,128]{2,1,0:T(8,128)(2,1)S(1)}, f32[2,256,128]{2,1,0:T(8,128)S(1)}, s32[1,8,128]{2,1,0:T(8,128)S(1)}) custom-call(bf16[32,24,128]{2,1,0:T(8,128)(2,1)S(1)} %all-to-all-done.got_ref, bf16[32,24,128]{2,1,0:T(8,128)(2,1)S(1)} %collective-permute-done.other_ref, ...), custom_call_target="tpu_custom_call" | custom-call | tf_op jit(solution)/shard_map/partials/pallas_call | solution.py:348
  21.6 0.3 %collective-permute-start.3 = (f32[80,128]{1,0:T(8,128)S(1)}, f32[80,128]{1,0:T(8,128)S(1)}, u32[]{:S(2)}, u32[]{:S(2)}) collective-permute-start(f32[80,128]{1,0:T(8,128)S(1)} %get-tuple-element.18.refs_0_), channel_id=1, source_target_pairs={{0,3},{1,2},{2,1},{3,0},{4,7},{5,6},{6,5},{7,4},{8,11},{9,10},{10,... | collective-permute-start | bytes 122888 | tf_op jit(solution)/shard_map/ppermute | solution.py:365
  21.9 1.3 %collective-permute-start.2 = (f32[80,128]{1,0:T(8,128)S(1)}, f32[80,128]{1,0:T(8,128)S(1)}, u32[]{:S(2)}, u32[]{:S(2)}) collective-permute-start(f32[80,128]{1,0:T(8,128)S(1)} %get-tuple-element.18.refs_0_), channel_id=1, source_target_pairs={{0,2},{1,3},{2,0},{3,1},{4,6},{5,7},{6,4},{7,5},{8,10},{9,11},{10,... | collective-permute-start | bytes 122888 | tf_op jit(solution)/shard_map/ppermute | solution.py:365
  23.2 0.7 %collective-permute-start.1 = (f32[80,128]{1,0:T(8,128)S(1)}, f32[80,128]{1,0:T(8,128)S(1)}, u32[]{:S(2)}, u32[]{:S(2)}) collective-permute-start(f32[80,128]{1,0:T(8,128)S(1)} %get-tuple-element.18.refs_0_), channel_id=1, source_target_pairs={{0,1},{1,0},{2,3},{3,2},{4,5},{5,4},{6,7},{7,6},{8,9},{9,8},{10,11... | collective-permute-start | bytes 122888 | tf_op jit(solution)/shard_map/ppermute | solution.py:365
  23.9 2.5 %user_rows.1 = f32[2048,128]{1,0:T(8,128)} custom-call(bf16[2048,128]{1,0:T(8,128)(2,1)} %u_hbm.1, bf16[2048,128]{1,0:T(8,128)(2,1)} %du_hbm.1, bf16[1,256,128]{2,1,0:T(8,128)(2,1)S(1)} %get-tuple-element.14.wt_ref, bf16[1,128,128]{2,1,0:T(8,128)(2,1)S(1)} %get-tuple-element.15.ww_ref, f32[2,256,128]{2,1,0:T(8,128)S(1)} %get-tuple-element.16.gh_ref, ...), custom_call_target="tpu_custom_call" | custom-call | tf_op jit(solution)/shard_map/user_rows/pallas_call | solution.py:366
  26.4 0.0 collective-permute-done.3.refs_3_
  26.4 0.0 collective-permute-done.2.refs_2_
  26.4 0.0 collective-permute-done.1.refs_1_
  26.4 0.6 %finish.1 = (f32[64,128]{1,0:T(8,128)}, f32[16,128]{1,0:T(8,128)}) custom-call(f32[80,128]{1,0:T(8,128)S(1)} %get-tuple-element.18.refs_0_, f32[80,128]{1,0:T(8,128)S(1)} %collective-permute-done.1.refs_1_, f32[80,128]{1,0:T(8,128)S(1)} %collective-permute-done.2.refs_2_, f32[80,128]{1,0:T(8,128)S(1)} %collective-permute-done.3.refs_3_), custom_call_target="tpu_custom_call" | custom-call | tf_op jit(solution)/shard_map/finish/pallas_call | solution.py:382
Async XLA Ops:
  2.9 16.3 %all-to-all-start = ((bf16[32,24,128]{2,1,0:T(8,128)(2,1)}), bf16[32,24,128]{2,1,0:T(8,128)(2,1)S(1)}, u32[]{:S(2)}, u32[]{:S(2)}) async-start(bf16[32,24,128]{2,1,0:T(8,128)(2,1)} %bitcast.1), calls=%async_computation | async-start | bytes 393216 | tf_op jit(solution)/shard_map/all_to_all | solution.py:343
  19.2 1.4 %collective-permute-start = (bf16[32,24,128]{2,1,0:T(8,128)(2,1)S(1)}, bf16[32,24,128]{2,1,0:T(8,128)(2,1)S(1)}, u32[]{:S(2)}, u32[]{:S(2)}) collective-permute-start(bf16[32,24,128]{2,1,0:T(8,128)(2,1)S(1)} %all-to-all-done.got_ref), channel_id=1, source_target_pairs={{0,1},{1,0},{2,3},{3,2},{4,5},{5,4},{6,7},{7,6},{8,9},{9,8},{10,11... | collective-permute-start | bytes 589832 | tf_op jit(solution)/shard_map/ppermute | solution.py:347
  21.6 4.7 %collective-permute-start.3 = (f32[80,128]{1,0:T(8,128)S(1)}, f32[80,128]{1,0:T(8,128)S(1)}, u32[]{:S(2)}, u32[]{:S(2)}) collective-permute-start(f32[80,128]{1,0:T(8,128)S(1)} %get-tuple-element.18.refs_0_), channel_id=1, source_target_pairs={{0,3},{1,2},{2,1},{3,0},{4,7},{5,6},{6,5},{7,4},{8,11},{9,10},{10,... | collective-permute-start | bytes 122888 | tf_op jit(solution)/shard_map/ppermute | solution.py:365
  21.9 4.4 %collective-permute-start.2 = (f32[80,128]{1,0:T(8,128)S(1)}, f32[80,128]{1,0:T(8,128)S(1)}, u32[]{:S(2)}, u32[]{:S(2)}) collective-permute-start(f32[80,128]{1,0:T(8,128)S(1)} %get-tuple-element.18.refs_0_), channel_id=1, source_target_pairs={{0,2},{1,3},{2,0},{3,1},{4,6},{5,7},{6,4},{7,5},{8,10},{9,11},{10,... | collective-permute-start | bytes 122888 | tf_op jit(solution)/shard_map/ppermute | solution.py:365
  23.2 3.2 %collective-permute-start.1 = (f32[80,128]{1,0:T(8,128)S(1)}, f32[80,128]{1,0:T(8,128)S(1)}, u32[]{:S(2)}, u32[]{:S(2)}) collective-permute-start(f32[80,128]{1,0:T(8,128)S(1)} %get-tuple-element.18.refs_0_), channel_id=1, source_target_pairs={{0,1},{1,0},{2,3},{3,2},{4,5},{5,4},{6,7},{7,6},{8,9},{9,8},{10,11... | collective-permute-start | bytes 122888 | tf_op jit(solution)/shard_map/ppermute | solution.py:365

commit v7 on v6

--- a/solution.py
+++ b/solution.py
@@ -128,6 +128,7 @@
     lane, row8 = iota((8, LANES), 1), iota((8, LANES), 0)
     slots = steps // peers
     even = me % 2 == 0
+    group = lane // slots % peers
 
     def sent(a, j, kind):
         here = a * peers + j
@@ -158,12 +159,14 @@
             sides[0].append(both[0])
             sides[1].append(both[1])
             mine = lane // steps == a
-            for j in range(peers):
-                at = 0 if j % 2 else 4
-                hit = mine & (row8 == at) & (lane // slots % peers == j)
-                found_m = found_m + jnp.where(hit, lasts[j], 0.0)
-                hit = mine & (row8 == at + 1) & (me == j)
-                found_g = found_g + jnp.where(hit, lasts[j], 0.0)
+            tile = lasts[0]
+            for j in range(1, peers):
+                tile = jnp.where(group == j, lasts[j], tile)
+            found_m = jnp.where(mine, tile, found_m)
+            own_list = got_ref[(base + a) * peers + me, part:, :].astype(F32)
+            found_g = jnp.where(mine, own_list, found_g)
+        found_m = jnp.where(row8 == jnp.where(group % 2 == 0, 4, 0), found_m, 0.0)
+        found_g = jnp.where(row8 == jnp.where(even, 5, 1), found_g, 0.0)
         w, dw = jnp.concatenate(sides[0], axis=0), jnp.concatenate(sides[1], axis=0)
         wt_ref[chunk] = jnp.concatenate([w, dw], axis=1).T.astype(BF16)
         ww_ref[chunk] = w.astype(BF16)

time: 27.5 us -> 27.5 us (level)
  no operation moved by 1% of the time
where the time goes in v7:
time: 27.5 us; the launch traced here: 27 us
  starting transfers between devices  9.29 us (34%)
  waiting for transfers between devices  8.33 us (30%)
  Pallas kernels  8.06 us (29%)
  between operations  1.34 us (5%)
    all_to_all x1, starting transfers between devices, body(): lax.all_to_all(packed.reshape(tm * peers, height, R), ('tm', 'user'), spl...  7.08 us
    all_to_all x1, waiting for transfers between devices, body(): lax.all_to_all(packed.reshape(tm * peers, height, R), ('tm', 'user'), spl...  6.89 us
    pallas_call x1, Pallas kernels, body(): pl.pallas_call(functools.partial(user_kernel, dims), out_shape=shape(user...  2.51 us
    pallas_call x1, Pallas kernels, body(): pl.pallas_call(gram_kernel, out_shape=near((groups, 2 * SUB * blocks, 2 *...  2.31 us
    ppermute x3, starting transfers between devices, body(): lax.ppermute(partial, 'user', [(i, i ^ d) for i in range(peers)])  2.21 us
    pallas_call x1, Pallas kernels, body(): pl.pallas_call(functools.partial(pack_kernel, dims), out_shape=shape((tm,...  1.6 us
    ppermute x1, waiting for transfers between devices, body(): other = lax.ppermute(got, 'user', [(i, i ^ 1) for i in range(peers)])  1.44 us
    pallas_call x1, Pallas kernels, body(): pl.pallas_call(functools.partial(partial_kernel, dims), out_shape=(near((...  1.02 us
  transfers between devices with their start and end apart: 5, of which 2 were waited for; matrix products, arithmetic and copies ran while one was open for 0% of the time, Pallas kernels for 18%

profile of v7, /device:TPU:1, one launch (start us, length us, event | category | flops | bytes accessed | tf_op | source)
XLA Modules:
  0.0 27.0 jit_solution(9602642419876644274)
XLA Ops:
  1.3 1.6 %pack.1 = bf16[8,4,24,128]{3,2,1,0:T(8,128)(2,1)} custom-call(bf16[64,128]{1,0:T(8,128)(2,1)} %v_ref.1, bf16[64,128]{1,0:T(8,128)(2,1)} %dv_ref.1, bf16[16,128]{1,0:T(8,128)(2,1)} %w_ref.1, bf16[16,128]{1,0:T(8,128)(2,1)} %dw_ref.1, s32[1,1,4,4]{3,2,1,0:T(4,128)} %send_ref.1, s32[1,1,16]{2,1,0:T(1,128)} %slot_ref.1, s32[1,1,16]{2,1,0:T(1,128)} %item_ref.1, ...), custom_call_target="tpu_custom_call" | custom-call | tf_op jit(solution)/shard_map/pack/pallas_call | solution.py:330
  2.9 7.1 %all-to-all-start = ((bf16[32,24,128]{2,1,0:T(8,128)(2,1)}), bf16[32,24,128]{2,1,0:T(8,128)(2,1)S(1)}, u32[]{:S(2)}, u32[]{:S(2)}) async-start(bf16[32,24,128]{2,1,0:T(8,128)(2,1)} %bitcast.1), calls=%async_computation | async-start | bytes 393216 | tf_op jit(solution)/shard_map/all_to_all | solution.py:346
  10.0 2.3 %grams.1.gram_ref = bf16[16,256,256]{2,1,0:T(8,128)(2,1)S(1)} custom-call(bf16[2048,128]{1,0:T(8,128)(2,1)} %u_hbm.1, bf16[2048,128]{1,0:T(8,128)(2,1)} %du_hbm.1), custom_call_target="tpu_custom_call" | custom-call | tf_op jit(solution)/shard_map/grams/pallas_call | solution.py:339
  12.3 6.9 %all-to-all-done.got_ref = bf16[32,24,128]{2,1,0:T(8,128)(2,1)S(1)} async-done(((bf16[32,24,128]{2,1,0:T(8,128)(2,1)}), bf16[32,24,128]{2,1,0:T(8,128)(2,1)S(1)}, u32[]{:S(2)}, u32[]{:S(2)}) %all-to-all-start) | async-done | bytes 196640 | tf_op jit(solution)/shard_map/all_to_all | solution.py:346
  19.2 0.0 collective-permute-start
  19.2 1.4 %collective-permute-done.other_ref = bf16[32,24,128]{2,1,0:T(8,128)(2,1)S(1)} collective-permute-done((bf16[32,24,128]{2,1,0:T(8,128)(2,1)S(1)}, bf16[32,24,128]{2,1,0:T(8,128)(2,1)S(1)}, u32[]{:S(2)}, u32[]{:S(2)}) %collective-permute-start) | collective-permute-done | bytes 196640 | tf_op jit(solution)/shard_map/ppermute | solution.py:350
  20.6 1.0 %partials.1 = (f32[80,128]{1,0:T(8,128)S(1)}, bf16[1,256,128]{2,1,0:T(8,128)(2,1)S(1)}, bf16[1,128,128]{2,1,0:T(8,128)(2,1)S(1)}, f32[2,256,128]{2,1,0:T(8,128)S(1)}, s32[1,8,128]{2,1,0:T(8,128)S(1)}) custom-call(bf16[32,24,128]{2,1,0:T(8,128)(2,1)S(1)} %all-to-all-done.got_ref, bf16[32,24,128]{2,1,0:T(8,128)(2,1)S(1)} %collective-permute-done.other_ref, ...), custom_call_target="tpu_custom_call" | custom-call | tf_op jit(solution)/shard_map/partials/pallas_call | solution.py:351
  21.6 0.3 %collective-permute-start.3 = (f32[80,128]{1,0:T(8,128)S(1)}, f32[80,128]{1,0:T(8,128)S(1)}, u32[]{:S(2)}, u32[]{:S(2)}) collective-permute-start(f32[80,128]{1,0:T(8,128)S(1)} %get-tuple-element.18.refs_0_), channel_id=1, source_target_pairs={{0,3},{1,2},{2,1},{3,0},{4,7},{5,6},{6,5},{7,4},{8,11},{9,10},{10,... | collective-permute-start | bytes 122888 | tf_op jit(solution)/shard_map/ppermute | solution.py:368
  21.9 1.3 %collective-permute-start.2 = (f32[80,128]{1,0:T(8,128)S(1)}, f32[80,128]{1,0:T(8,128)S(1)}, u32[]{:S(2)}, u32[]{:S(2)}) collective-permute-start(f32[80,128]{1,0:T(8,128)S(1)} %get-tuple-element.18.refs_0_), channel_id=1, source_target_pairs={{0,2},{1,3},{2,0},{3,1},{4,6},{5,7},{6,4},{7,5},{8,10},{9,11},{10,... | collective-permute-start | bytes 122888 | tf_op jit(solution)/shard_map/ppermute | solution.py:368
  23.2 0.7 %collective-permute-start.1 = (f32[80,128]{1,0:T(8,128)S(1)}, f32[80,128]{1,0:T(8,128)S(1)}, u32[]{:S(2)}, u32[]{:S(2)}) collective-permute-start(f32[80,128]{1,0:T(8,128)S(1)} %get-tuple-element.18.refs_0_), channel_id=1, source_target_pairs={{0,1},{1,0},{2,3},{3,2},{4,5},{5,4},{6,7},{7,6},{8,9},{9,8},{10,11... | collective-permute-start | bytes 122888 | tf_op jit(solution)/shard_map/ppermute | solution.py:368
  23.8 2.5 %user_rows.1 = f32[2048,128]{1,0:T(8,128)} custom-call(bf16[2048,128]{1,0:T(8,128)(2,1)} %u_hbm.1, bf16[2048,128]{1,0:T(8,128)(2,1)} %du_hbm.1, bf16[1,256,128]{2,1,0:T(8,128)(2,1)S(1)} %get-tuple-element.14.wt_ref, bf16[1,128,128]{2,1,0:T(8,128)(2,1)S(1)} %get-tuple-element.15.ww_ref, f32[2,256,128]{2,1,0:T(8,128)S(1)} %get-tuple-element.16.gh_ref, ...), custom_call_target="tpu_custom_call" | custom-call | tf_op jit(solution)/shard_map/user_rows/pallas_call | solution.py:369
  26.4 0.0 collective-permute-done.3.refs_3_
  26.4 0.0 collective-permute-done.2.refs_2_
  26.4 0.0 collective-permute-done.1.refs_1_
  26.4 0.6 %finish.1 = (f32[64,128]{1,0:T(8,128)}, f32[16,128]{1,0:T(8,128)}) custom-call(f32[80,128]{1,0:T(8,128)S(1)} %get-tuple-element.18.refs_0_, f32[80,128]{1,0:T(8,128)S(1)} %collective-permute-done.1.refs_1_, f32[80,128]{1,0:T(8,128)S(1)} %collective-permute-done.2.refs_2_, f32[80,128]{1,0:T(8,128)S(1)} %collective-permute-done.3.refs_3_), custom_call_target="tpu_custom_call" | custom-call | tf_op jit(solution)/shard_map/finish/pallas_call | solution.py:385
Async XLA Ops:
  2.9 16.3 %all-to-all-start = ((bf16[32,24,128]{2,1,0:T(8,128)(2,1)}), bf16[32,24,128]{2,1,0:T(8,128)(2,1)S(1)}, u32[]{:S(2)}, u32[]{:S(2)}) async-start(bf16[32,24,128]{2,1,0:T(8,128)(2,1)} %bitcast.1), calls=%async_computation | async-start | bytes 393216 | tf_op jit(solution)/shard_map/all_to_all | solution.py:346
  19.2 1.4 %collective-permute-start = (bf16[32,24,128]{2,1,0:T(8,128)(2,1)S(1)}, bf16[32,24,128]{2,1,0:T(8,128)(2,1)S(1)}, u32[]{:S(2)}, u32[]{:S(2)}) collective-permute-start(bf16[32,24,128]{2,1,0:T(8,128)(2,1)S(1)} %all-to-all-done.got_ref), channel_id=1, source_target_pairs={{0,1},{1,0},{2,3},{3,2},{4,5},{5,4},{6,7},{7,6},{8,9},{9,8},{10,11... | collective-permute-start | bytes 589832 | tf_op jit(solution)/shard_map/ppermute | solution.py:350
  21.6 4.7 %collective-permute-start.3 = (f32[80,128]{1,0:T(8,128)S(1)}, f32[80,128]{1,0:T(8,128)S(1)}, u32[]{:S(2)}, u32[]{:S(2)}) collective-permute-start(f32[80,128]{1,0:T(8,128)S(1)} %get-tuple-element.18.refs_0_), channel_id=1, source_target_pairs={{0,3},{1,2},{2,1},{3,0},{4,7},{5,6},{6,5},{7,4},{8,11},{9,10},{10,... | collective-permute-start | bytes 122888 | tf_op jit(solution)/shard_map/ppermute | solution.py:368
  21.9 4.4 %collective-permute-start.2 = (f32[80,128]{1,0:T(8,128)S(1)}, f32[80,128]{1,0:T(8,128)S(1)}, u32[]{:S(2)}, u32[]{:S(2)}) collective-permute-start(f32[80,128]{1,0:T(8,128)S(1)} %get-tuple-element.18.refs_0_), channel_id=1, source_target_pairs={{0,2},{1,3},{2,0},{3,1},{4,6},{5,7},{6,4},{7,5},{8,10},{9,11},{10,... | collective-permute-start | bytes 122888 | tf_op jit(solution)/shard_map/ppermute | solution.py:368
  23.2 3.2 %collective-permute-start.1 = (f32[80,128]{1,0:T(8,128)S(1)}, f32[80,128]{1,0:T(8,128)S(1)}, u32[]{:S(2)}, u32[]{:S(2)}) collective-permute-start(f32[80,128]{1,0:T(8,128)S(1)} %get-tuple-element.18.refs_0_), channel_id=1, source_target_pairs={{0,1},{1,0},{2,3},{3,2},{4,5},{5,4},{6,7},{7,6},{8,9},{9,8},{10,11... | collective-permute-start | bytes 122888 | tf_op jit(solution)/shard_map/ppermute | solution.py:368

commit v8 on v7

--- a/solution.py
+++ b/solution.py
@@ -378,7 +378,7 @@
             pltpu.VMEM((LANES // steps, 2 * R, R), F32),
             pltpu.VMEM((blocks, R, 2 * R), F32),
             pltpu.SemaphoreType.DMA((2,)),
-            pltpu.SemaphoreType.DMA((4,)),
+            pltpu.SemaphoreType.DMA((8,)),
         ],
         name="user_rows",
     )(user_factor, user_tangent, *held(wt, ww, gh, listed))

time: 27.5 us -> 27.5 us (level)
  no operation moved by 1% of the time
where the time goes in v8:
time: 27.5 us; the launch traced here: 27 us
  starting transfers between devices  9.29 us (34%)
  waiting for transfers between devices  8.33 us (30%)
  Pallas kernels  8.05 us (29%)
  between operations  1.34 us (5%)
    all_to_all x1, starting transfers between devices, body(): lax.all_to_all(packed.reshape(tm * peers, height, R), ('tm', 'user'), spl...  7.08 us
    all_to_all x1, waiting for transfers between devices, body(): lax.all_to_all(packed.reshape(tm * peers, height, R), ('tm', 'user'), spl...  6.89 us
    pallas_call x1, Pallas kernels, body(): pl.pallas_call(functools.partial(user_kernel, dims), out_shape=shape(user...  2.5 us
    pallas_call x1, Pallas kernels, body(): pl.pallas_call(gram_kernel, out_shape=near((groups, 2 * SUB * blocks, 2 *...  2.31 us
    ppermute x3, starting transfers between devices, body(): lax.ppermute(partial, 'user', [(i, i ^ d) for i in range(peers)])  2.21 us
    pallas_call x1, Pallas kernels, body(): pl.pallas_call(functools.partial(pack_kernel, dims), out_shape=shape((tm,...  1.6 us
    ppermute x1, waiting for transfers between devices, body(): other = lax.ppermute(got, 'user', [(i, i ^ 1) for i in range(peers)])  1.44 us
    pallas_call x1, Pallas kernels, body(): pl.pallas_call(functools.partial(partial_kernel, dims), out_shape=(near((...  1.02 us
  transfers between devices with their start and end apart: 5, of which 2 were waited for; matrix products, arithmetic and copies ran while one was open for 0% of the time, Pallas kernels for 18%

profile of v8, /device:TPU:1, one launch (start us, length us, event | category | flops | bytes accessed | tf_op | source)
XLA Modules:
  0.0 27.0 jit_solution(1438718949820039044)
XLA Ops:
  1.3 1.6 %pack.1 = bf16[8,4,24,128]{3,2,1,0:T(8,128)(2,1)} custom-call(bf16[64,128]{1,0:T(8,128)(2,1)} %v_ref.1, bf16[64,128]{1,0:T(8,128)(2,1)} %dv_ref.1, bf16[16,128]{1,0:T(8,128)(2,1)} %w_ref.1, bf16[16,128]{1,0:T(8,128)(2,1)} %dw_ref.1, s32[1,1,4,4]{3,2,1,0:T(4,128)} %send_ref.1, s32[1,1,16]{2,1,0:T(1,128)} %slot_ref.1, s32[1,1,16]{2,1,0:T(1,128)} %item_ref.1, ...), custom_call_target="tpu_custom_call" | custom-call | tf_op jit(solution)/shard_map/pack/pallas_call | solution.py:330
  2.9 7.1 %all-to-all-start = ((bf16[32,24,128]{2,1,0:T(8,128)(2,1)}), bf16[32,24,128]{2,1,0:T(8,128)(2,1)S(1)}, u32[]{:S(2)}, u32[]{:S(2)}) async-start(bf16[32,24,128]{2,1,0:T(8,128)(2,1)} %bitcast.1), calls=%async_computation | async-start | bytes 393216 | tf_op jit(solution)/shard_map/all_to_all | solution.py:346
  10.0 2.3 %grams.1.gram_ref = bf16[16,256,256]{2,1,0:T(8,128)(2,1)S(1)} custom-call(bf16[2048,128]{1,0:T(8,128)(2,1)} %u_hbm.1, bf16[2048,128]{1,0:T(8,128)(2,1)} %du_hbm.1), custom_call_target="tpu_custom_call" | custom-call | tf_op jit(solution)/shard_map/grams/pallas_call | solution.py:339
  12.3 6.9 %all-to-all-done.got_ref = bf16[32,24,128]{2,1,0:T(8,128)(2,1)S(1)} async-done(((bf16[32,24,128]{2,1,0:T(8,128)(2,1)}), bf16[32,24,128]{2,1,0:T(8,128)(2,1)S(1)}, u32[]{:S(2)}, u32[]{:S(2)}) %all-to-all-start) | async-done | bytes 196640 | tf_op jit(solution)/shard_map/all_to_all | solution.py:346
  19.2 0.0 collective-permute-start
  19.2 1.4 %collective-permute-done.other_ref = bf16[32,24,128]{2,1,0:T(8,128)(2,1)S(1)} collective-permute-done((bf16[32,24,128]{2,1,0:T(8,128)(2,1)S(1)}, bf16[32,24,128]{2,1,0:T(8,128)(2,1)S(1)}, u32[]{:S(2)}, u32[]{:S(2)}) %collective-permute-start) | collective-permute-done | bytes 196640 | tf_op jit(solution)/shard_map/ppermute | solution.py:350
  20.6 1.0 %partials.1 = (f32[80,128]{1,0:T(8,128)S(1)}, bf16[1,256,128]{2,1,0:T(8,128)(2,1)S(1)}, bf16[1,128,128]{2,1,0:T(8,128)(2,1)S(1)}, f32[2,256,128]{2,1,0:T(8,128)S(1)}, s32[1,8,128]{2,1,0:T(8,128)S(1)}) custom-call(bf16[32,24,128]{2,1,0:T(8,128)(2,1)S(1)} %all-to-all-done.got_ref, bf16[32,24,128]{2,1,0:T(8,128)(2,1)S(1)} %collective-permute-done.other_ref, ...), custom_call_target="tpu_custom_call" | custom-call | tf_op jit(solution)/shard_map/partials/pallas_call | solution.py:351
  21.6 0.3 %collective-permute-start.3 = (f32[80,128]{1,0:T(8,128)S(1)}, f32[80,128]{1,0:T(8,128)S(1)}, u32[]{:S(2)}, u32[]{:S(2)}) collective-permute-start(f32[80,128]{1,0:T(8,128)S(1)} %get-tuple-element.18.refs_0_), channel_id=1, source_target_pairs={{0,3},{1,2},{2,1},{3,0},{4,7},{5,6},{6,5},{7,4},{8,11},{9,10},{10,... | collective-permute-start | bytes 122888 | tf_op jit(solution)/shard_map/ppermute | solution.py:368
  21.9 1.3 %collective-permute-start.2 = (f32[80,128]{1,0:T(8,128)S(1)}, f32[80,128]{1,0:T(8,128)S(1)}, u32[]{:S(2)}, u32[]{:S(2)}) collective-permute-start(f32[80,128]{1,0:T(8,128)S(1)} %get-tuple-element.18.refs_0_), channel_id=1, source_target_pairs={{0,2},{1,3},{2,0},{3,1},{4,6},{5,7},{6,4},{7,5},{8,10},{9,11},{10,... | collective-permute-start | bytes 122888 | tf_op jit(solution)/shard_map/ppermute | solution.py:368
  23.2 0.7 %collective-permute-start.1 = (f32[80,128]{1,0:T(8,128)S(1)}, f32[80,128]{1,0:T(8,128)S(1)}, u32[]{:S(2)}, u32[]{:S(2)}) collective-permute-start(f32[80,128]{1,0:T(8,128)S(1)} %get-tuple-element.18.refs_0_), channel_id=1, source_target_pairs={{0,1},{1,0},{2,3},{3,2},{4,5},{5,4},{6,7},{7,6},{8,9},{9,8},{10,11... | collective-permute-start | bytes 122888 | tf_op jit(solution)/shard_map/ppermute | solution.py:368
  23.8 2.5 %user_rows.1 = f32[2048,128]{1,0:T(8,128)} custom-call(bf16[2048,128]{1,0:T(8,128)(2,1)} %u_hbm.1, bf16[2048,128]{1,0:T(8,128)(2,1)} %du_hbm.1, bf16[1,256,128]{2,1,0:T(8,128)(2,1)S(1)} %get-tuple-element.14.wt_ref, bf16[1,128,128]{2,1,0:T(8,128)(2,1)S(1)} %get-tuple-element.15.ww_ref, f32[2,256,128]{2,1,0:T(8,128)S(1)} %get-tuple-element.16.gh_ref, ...), custom_call_target="tpu_custom_call" | custom-call | tf_op jit(solution)/shard_map/user_rows/pallas_call | solution.py:369
  26.4 0.0 collective-permute-done.3.refs_3_
  26.4 0.0 collective-permute-done.2.refs_2_
  26.4 0.0 collective-permute-done.1.refs_1_
  26.4 0.6 %finish.1 = (f32[64,128]{1,0:T(8,128)}, f32[16,128]{1,0:T(8,128)}) custom-call(f32[80,128]{1,0:T(8,128)S(1)} %get-tuple-element.18.refs_0_, f32[80,128]{1,0:T(8,128)S(1)} %collective-permute-done.1.refs_1_, f32[80,128]{1,0:T(8,128)S(1)} %collective-permute-done.2.refs_2_, f32[80,128]{1,0:T(8,128)S(1)} %collective-permute-done.3.refs_3_), custom_call_target="tpu_custom_call" | custom-call | tf_op jit(solution)/shard_map/finish/pallas_call | solution.py:385
Async XLA Ops:
  2.9 16.3 %all-to-all-start = ((bf16[32,24,128]{2,1,0:T(8,128)(2,1)}), bf16[32,24,128]{2,1,0:T(8,128)(2,1)S(1)}, u32[]{:S(2)}, u32[]{:S(2)}) async-start(bf16[32,24,128]{2,1,0:T(8,128)(2,1)} %bitcast.1), calls=%async_computation | async-start | bytes 393216 | tf_op jit(solution)/shard_map/all_to_all | solution.py:346
  19.2 1.4 %collective-permute-start = (bf16[32,24,128]{2,1,0:T(8,128)(2,1)S(1)}, bf16[32,24,128]{2,1,0:T(8,128)(2,1)S(1)}, u32[]{:S(2)}, u32[]{:S(2)}) collective-permute-start(bf16[32,24,128]{2,1,0:T(8,128)(2,1)S(1)} %all-to-all-done.got_ref), channel_id=1, source_target_pairs={{0,1},{1,0},{2,3},{3,2},{4,5},{5,4},{6,7},{7,6},{8,9},{9,8},{10,11... | collective-permute-start | bytes 589832 | tf_op jit(solution)/shard_map/ppermute | solution.py:350
  21.6 4.7 %collective-permute-start.3 = (f32[80,128]{1,0:T(8,128)S(1)}, f32[80,128]{1,0:T(8,128)S(1)}, u32[]{:S(2)}, u32[]{:S(2)}) collective-permute-start(f32[80,128]{1,0:T(8,128)S(1)} %get-tuple-element.18.refs_0_), channel_id=1, source_target_pairs={{0,3},{1,2},{2,1},{3,0},{4,7},{5,6},{6,5},{7,4},{8,11},{9,10},{10,... | collective-permute-start | bytes 122888 | tf_op jit(solution)/shard_map/ppermute | solution.py:368
  21.9 4.4 %collective-permute-start.2 = (f32[80,128]{1,0:T(8,128)S(1)}, f32[80,128]{1,0:T(8,128)S(1)}, u32[]{:S(2)}, u32[]{:S(2)}) collective-permute-start(f32[80,128]{1,0:T(8,128)S(1)} %get-tuple-element.18.refs_0_), channel_id=1, source_target_pairs={{0,2},{1,3},{2,0},{3,1},{4,6},{5,7},{6,4},{7,5},{8,10},{9,11},{10,... | collective-permute-start | bytes 122888 | tf_op jit(solution)/shard_map/ppermute | solution.py:368
  23.2 3.2 %collective-permute-start.1 = (f32[80,128]{1,0:T(8,128)S(1)}, f32[80,128]{1,0:T(8,128)S(1)}, u32[]{:S(2)}, u32[]{:S(2)}) collective-permute-start(f32[80,128]{1,0:T(8,128)S(1)} %get-tuple-element.18.refs_0_), channel_id=1, source_target_pairs={{0,1},{1,0},{2,3},{3,2},{4,5},{5,4},{6,7},{7,6},{8,9},{9,8},{10,11... | collective-permute-start | bytes 122888 | tf_op jit(solution)/shard_map/ppermute | solution.py:368
